TPU v7x, 768 devices: a whole 4x8x12 slice. The times are simulated.
768 devices in a mesh: pipe: 2 (over core), dp: 48 (over z, x), tensor: 8 (over y).
Axes of the slice: x: 4, y: 8, z: 12, core: 2. Of those that a mesh axis runs over, the one named last changes fastest.
Arguments:
- stream_in: bfloat16 [2, 24576, 4096], P('pipe', 'dp', 'tensor'), may hold values from -4.5 to 4.5
- saved_in: bfloat16 [2, 24576, 4096], P('pipe', 'dp', 'tensor'), may hold values from -4.5 to 4.5
- grad_out: bfloat16 [2, 24576, 4096], P('pipe', 'dp', 'tensor'), may hold values from -6 to 6
- mem_keys: bfloat16 [2, 96, 8, 4096], P('pipe', 'dp', None, 'tensor'), may hold values from -4.5 to 4.5
- mem_values: bfloat16 [2, 96, 8, 4096], P('pipe', 'dp', None, 'tensor'), may hold values from -6 to 6
- owner_map: int32 [96], replicated, may hold values from 0 to 95, as said below
- block_ids: int32 [2, 2, 48, 16], P(None, 'pipe', 'dp'), may hold values from 0 to 95, as said below
Outputs:
- next_input: bfloat16 [2, 24576, 4096], P('pipe', 'dp', 'tensor')
- grad_back: bfloat16 [2, 24576, 4096], P('pipe', 'dp', 'tensor')
- key_grad: bfloat16 [2, 96, 8, 4096], P('pipe', 'dp', None, 'tensor')
- value_grad: bfloat16 [2, 96, 8, 4096], P('pipe', 'dp', None, 'tensor')
Inputs may be any that keep to these rules, and one draw needn't show every extreme that they name: `owner_map`: A permutation of the block ids; location loc lies with replica loc // 2 in slot loc % 2. `block_ids`: for each section and replica, the 32 ids of both micro-batches together lie with 32 different replicas, so at most one block is requested from one replica; in every section one replica is asked for a block by every replica, itself included.
All inputs are finite; a program needn't handle non-finite values.
Results may differ from a plain program's by a relative error of at most 0.0057.
Values may be sent and summed in bfloat16 or wider, within the bound.
A program may use at most 32 MiB of HBM per device.

v0:
```python
import math

import jax
import jax.numpy as jnp
from jax import lax
from jax.sharding import PartitionSpec as P

HEAD_DIM = 128


def from_behind(x, axis, by):
    peers = lax.axis_size(axis)
    pairs = [(i, i + by) for i in range(peers) if 0 <= i + by < peers]
    return lax.ppermute(x, axis, pairs)


def forward_part(inputs, memory_keys, memory_values):
    rows = inputs.shape[0]
    heads_count = inputs.shape[1] // HEAD_DIM
    scale = 1.0 / math.sqrt(HEAD_DIM)
    queries = inputs.reshape(rows, heads_count, HEAD_DIM)
    key_rows = memory_keys.reshape(-1, heads_count, HEAD_DIM)
    value_rows = memory_values.reshape(-1, heads_count, HEAD_DIM)
    scores = (
        jnp.einsum("thd,khd->htk", queries, key_rows, preferred_element_type=jnp.float32) * scale
    )
    exponent = jnp.exp(scores - jnp.max(scores, axis=-1, keepdims=True))
    weights = exponent / jnp.sum(exponent, axis=-1, keepdims=True)
    rounded = weights.astype(jnp.bfloat16)
    attended = jnp.einsum(
        "htk,khd->thd", rounded, value_rows, preferred_element_type=jnp.float32
    ).reshape(rows, -1)
    return (queries, key_rows, value_rows, weights, rounded, attended)


def backward_part(inputs, grads, memory_keys, memory_values):
    queries, key_rows, value_rows, weights, rounded, attended = forward_part(
        inputs, memory_keys, memory_values
    )
    rows = inputs.shape[0]
    heads_count = queries.shape[1]
    scale = 1.0 / math.sqrt(HEAD_DIM)
    grad_rows = grads.reshape(rows, heads_count, HEAD_DIM)
    grad_weights = jnp.einsum(
        "thd,khd->htk", grad_rows, value_rows, preferred_element_type=jnp.float32
    )
    centre = jnp.sum(weights * grad_weights, axis=-1, keepdims=True)
    grad_scores = (weights * (grad_weights - centre) * scale).astype(jnp.bfloat16)
    grad_queries = jnp.einsum(
        "htk,khd->thd", grad_scores, key_rows, preferred_element_type=jnp.float32
    ).reshape(rows, -1)
    key_terms = jnp.einsum("htk,thd->khd", grad_scores, queries, preferred_element_type=jnp.float32)
    value_terms = jnp.einsum("htk,thd->khd", rounded, grad_rows, preferred_element_type=jnp.float32)
    input_grad = (grads.astype(jnp.float32) + grad_queries).astype(jnp.bfloat16)
    key_count = key_rows.shape[0]
    return (
        input_grad,
        key_terms.reshape(key_count, -1).astype(jnp.bfloat16),
        value_terms.reshape(key_count, -1).astype(jnp.bfloat16),
    )


def local(stream_in, saved_in, grad_out, mem_keys, mem_values, owner_map, block_ids):
    replicas = lax.axis_size("dp")
    local_blocks = mem_keys.shape[1]
    block_rows = mem_keys.shape[2]
    width = stream_in.shape[2]
    table_size = owner_map.shape[0]
    requested = block_ids.reshape(-1)
    picks = requested.shape[0]
    half = picks // 2
    matches = requested[:, None] == jnp.arange(table_size, dtype=jnp.int32)[None, :]
    places = jnp.sum(jnp.where(matches, owner_map[None, :], 0), axis=1)
    owners = places // local_blocks
    slot_ids = places % local_blocks
    owner_hits = owners[:, None] == jnp.arange(replicas, dtype=jnp.int32)[None, :]
    served = None
    wanted = jnp.sum(jnp.where(owner_hits, slot_ids[:, None], 0), axis=0)
    served = lax.all_to_all(
        wanted.reshape(replicas, 1), "dp", split_axis=0, concat_axis=0, tiled=True
    ).reshape(replicas)
    out_keys = jnp.take(mem_keys[0], served, axis=0)
    out_values = jnp.take(mem_values[0], served, axis=0)
    got_keys, got_values = (
        lax.all_to_all(out_keys, "dp", split_axis=0, concat_axis=0, tiled=True),
        lax.all_to_all(out_values, "dp", split_axis=0, concat_axis=0, tiled=True),
    )
    fetched_keys = jnp.take(got_keys, owners, axis=0)
    fetched_values = jnp.take(got_values, owners, axis=0)
    forward_keys = fetched_keys[:half].reshape(-1, width)
    forward_values = fetched_values[:half].reshape(-1, width)
    backward_keys = fetched_keys[half:].reshape(-1, width)
    backward_values = fetched_values[half:].reshape(-1, width)
    attended = forward_part(stream_in[0], forward_keys, forward_values)[5]
    section_out = (stream_in[0].astype(jnp.float32) + attended).astype(jnp.bfloat16)
    next_input = from_behind(section_out[None], "pipe", 1)
    input_grad, key_terms, value_terms = backward_part(
        saved_in[0], grad_out[0], backward_keys, backward_values
    )
    grad_back = from_behind(input_grad[None], "pipe", -1)
    key_blocks = key_terms.reshape(half, block_rows, width)
    value_blocks = value_terms.reshape(half, block_rows, width)
    back_hits = owner_hits[half:].astype(jnp.bfloat16)
    send_keys = jnp.einsum(
        "ro,rtf->otf", back_hits, key_blocks, preferred_element_type=jnp.float32
    ).astype(jnp.bfloat16)
    send_values = jnp.einsum(
        "ro,rtf->otf", back_hits, value_blocks, preferred_element_type=jnp.float32
    ).astype(jnp.bfloat16)
    recv_keys, recv_values = (
        lax.all_to_all(send_keys, "dp", split_axis=0, concat_axis=0, tiled=True),
        lax.all_to_all(send_values, "dp", split_axis=0, concat_axis=0, tiled=True),
    )
    slot_hits = (served[:, None] == jnp.arange(local_blocks, dtype=jnp.int32)[None, :]).astype(
        jnp.bfloat16
    )
    key_grad = jnp.einsum(
        "sm,stf->mtf", slot_hits, recv_keys, preferred_element_type=jnp.float32
    ).astype(jnp.bfloat16)
    value_grad = jnp.einsum(
        "sm,stf->mtf", slot_hits, recv_values, preferred_element_type=jnp.float32
    ).astype(jnp.bfloat16)
    return (next_input, grad_back, key_grad[None], value_grad[None])


def solution(mesh):
    in_specs = (
        P("pipe", "dp", "tensor"),
        P("pipe", "dp", "tensor"),
        P("pipe", "dp", "tensor"),
        P("pipe", "dp", None, "tensor"),
        P("pipe", "dp", None, "tensor"),
        P(),
        P(None, "pipe", "dp", None),
    )
    out_specs = (
        P("pipe", "dp", "tensor"),
        P("pipe", "dp", "tensor"),
        P("pipe", "dp", None, "tensor"),
        P("pipe", "dp", None, "tensor"),
    )
    return jax.shard_map(local, mesh=mesh, in_specs=in_specs, out_specs=out_specs, check_vma=False)
```

profile of v0, /device:TPU:56, one launch (start us, length us, event | category | flops | bytes accessed | tf_op | source)
XLA Modules:
  0.0 150.5 jit_solution(6716419985839900822)
XLA Ops:
  0.7 0.5 broadcast.126
  1.3 0.7 reduce.4
  2.1 0.6 copy-done.17
  3.1 30.2 %all_to_all.29 = s32[48,1,1]{2,1,0:T(1,128)S(1)} all-to-all(s32[48,1,1]{2,1,0:T(1,128)S(1)} %copy.92), channel_id=1, replica_groups=mesh['pipe'=2,'dp'=48,'tensor'=8] {'dp'}, dimensions={0} | all-to-all | bytes 384 | tf_op jit(solution)/shard_map/all_to_all | solution.py:79
  33.2 0.9 reduce.1
  34.2 0.5 copy-done.14
  34.7 0.6 gather_fusion.2
  35.4 0.6 gather_fusion
  36.0 0.9 broadcast_select_fusion.1
  36.9 24.4 %all_to_all.30 = bf16[48,8,512]{2,1,0:T(8,128)(2,1)S(1)} all-to-all(bf16[48,8,512]{2,1,0:T(8,128)(2,1)S(1)} %get-tuple-element.34), channel_id=1, replica_groups=mesh['pipe'=2,'dp'=48,'tensor'=8] {'dp'}, dimensions={0} | all-to-all | bytes 786432 | tf_op jit(solution)/shard_map/all_to_all | solution.py:86
  61.3 5.2 %all-to-all-start.2 = ((bf16[48,8,512]{2,1,0:T(8,128)(2,1)}), bf16[48,8,512]{2,1,0:T(8,128)(2,1)S(1)}, u32[]{:S(2)}, u32[]{:S(2)}) async-start(bf16[48,8,512]{2,1,0:T(8,128)(2,1)} %get-tuple-element.35), calls=%async_computation.2 | async-start | bytes 786432 | tf_op jit(solution)/shard_map/all_to_all | solution.py:85
  66.6 0.9 reshape_squeeze.10
  67.8 0.9 copy-done.3
  68.8 0.7 iota_compare_fusion
  69.5 0.6 gather_fusion.1
  70.1 16.7 %all-to-all-done.2 = bf16[48,8,512]{2,1,0:T(8,128)(2,1)S(1)} async-done(((bf16[48,8,512]{2,1,0:T(8,128)(2,1)}), bf16[48,8,512]{2,1,0:T(8,128)(2,1)S(1)}, u32[]{:S(2)}, u32[]{:S(2)}) %all-to-all-start.2) | async-done | bytes 393248 | tf_op jit(solution)/shard_map/all_to_all | solution.py:85
  86.7 0.6 gather_fusion.3
  87.6 0.6 copy-done.8
  88.2 1.1 fusion.60
  89.3 1.2 fusion.11
  90.5 0.7 reshape_reshape.15
  91.2 0.7 reshape_reshape.12
  92.1 1.5 fusion.65
  93.6 1.5 %fusion.14 = bf16[128,4,128]{2,0,1:T(8,128)(2,1)S(1)} fusion(bf16[512,4,128]{2,1,0:T(4,128)(2,1)S(1)} %reshape_squeeze.11, f32[4,512,128]{1,2,0:T(8,128)} %get-tuple-element.37, f32[4,512]{1,0:T(4,128)S(1)} %get-tuple-element.36), kind=kOutput, calls=%fused_computation.25 | convolution fusion | flops 67698688 | bytes 1712128 | tf_op jit(solution)/shard_map/htk,thd->khd/dot_general | solution.py:53
  95.3 0.6 copy-done.12
  95.9 0.3 convolution_convert_fusion
  96.2 1.0 copy.113
  97.2 5.4 %all-to-all-start.4 = ((bf16[48,8,512]{2,1,0:T(8,128)(2,1)}), bf16[48,8,512]{2,1,0:T(8,128)(2,1)S(1)}, u32[]{:S(2)}, u32[]{:S(2)}) async-start(bf16[48,8,512]{2,1,0:T(8,128)(2,1)} %copy.113), calls=%async_computation.4 | async-start | bytes 786432 | tf_op jit(solution)/shard_map/all_to_all | solution.py:112
  102.6 1.5 fusion.26
  104.1 1.6 %copy.97 = f32[1,512,512]{2,1,0:T(8,128)S(1)} copy(f32[1,512,512]{1,2,0:T(8,128)} %bitcast.48) | data formatting | bytes 2097152 | tf_op jit(solution)/shard_map/reshape | solution.py:32
  105.7 1.0 add_convert_fusion.1
  106.6 1.4 collective-permute-start
  108.1 0.3 convolution_bitcast_fusion
  108.4 2.2 %fusion.13 = bf16[128,4,128]{2,0,1:T(8,128)(2,1)S(1)} fusion(f32[4,512,128]{1,2,0:T(8,128)S(1)} %convolution_bitcast_fusion, bf16[512,4,128]{2,1,0:T(4,128)(2,1)S(1)} %copy-done.6, f32[4,512,128]{1,2,0:T(8,128)} %get-tuple-element.37, f32[4,512]{1,0:T(4,128)} %copy-done.18), kind=kOutput, calls=%fused_computation.24 | convolution fusion | flops 69011584 | bytes 2760704 | tf_op jit(solution)/shard_map/htk,thd->khd/dot_general | solution.py:52
  110.8 0.6 copy-done.13
  111.4 0.3 convolution_convert_fusion.1
  111.7 1.0 copy.108
  112.7 10.0 %all-to-all-done.4 = bf16[48,8,512]{2,1,0:T(8,128)(2,1)S(1)} async-done(((bf16[48,8,512]{2,1,0:T(8,128)(2,1)}), bf16[48,8,512]{2,1,0:T(8,128)(2,1)S(1)}, u32[]{:S(2)}, u32[]{:S(2)}) %all-to-all-start.4) | async-done | bytes 393248 | tf_op jit(solution)/shard_map/all_to_all | solution.py:112
  122.7 5.2 %all-to-all-start.3 = ((bf16[48,8,512]{2,1,0:T(8,128)(2,1)}), bf16[48,8,512]{2,1,0:T(8,128)(2,1)S(1)}, u32[]{:S(2)}, u32[]{:S(2)}) async-start(bf16[48,8,512]{2,1,0:T(8,128)(2,1)} %copy.108), calls=%async_computation.3 | async-start | bytes 786432 | tf_op jit(solution)/shard_map/all_to_all | solution.py:111
  127.9 3.1 %fusion.17 = f32[4,128,512]{2,1,0:T(8,128)} fusion(bf16[128,4,128]{0,2,1:T(8,128)(2,1)S(1)} %copy-done.10, f32[4,512,128]{1,2,0:T(8,128)S(1)} %convolution_bitcast_fusion, f32[4,512,128]{1,2,0:T(8,128)} %get-tuple-element.37, f32[4,512]{1,0:T(4,128)S(1)} %copy-done.19), kind=kOutput, calls=%fused_computation.33 | convolution fusion | flops 68946048 | bytes 3284992 | tf_op jit(solution)/shard_map/htk,khd->thd/dot_general | solution.py:49
  131.1 1.6 %copy.104 = f32[1,512,512]{2,1,0:T(8,128)S(1)} copy(f32[1,512,512]{1,2,0:T(8,128)} %bitcast.47) | data formatting | bytes 2097152 | tf_op jit(solution)/shard_map/reshape | solution.py:51
  132.8 1.3 collective-permute-start.1
  134.1 2.5 %collective-permute-done.1 = bf16[1,512,512]{2,1,0:T(8,128)(2,1)S(1)} collective-permute-done((bf16[1,512,512]{2,1,0:T(8,128)(2,1)S(1)}, bf16[1,512,512]{2,1,0:T(8,128)(2,1)S(1)}, u32[]{:S(2)}, u32[]{:S(2)}) %collective-permute-start.1) | collective-permute-done | bytes 524320 | tf_op jit(solution)/shard_map/ppermute | solution.py:14
  136.8 0.6 copy.116
  137.4 10.6 %all-to-all-done.3 = bf16[48,8,512]{2,1,0:T(8,128)(2,1)S(1)} async-done(((bf16[48,8,512]{2,1,0:T(8,128)(2,1)}), bf16[48,8,512]{2,1,0:T(8,128)(2,1)S(1)}, u32[]{:S(2)}, u32[]{:S(2)}) %all-to-all-start.3) | async-done | bytes 393248 | tf_op jit(solution)/shard_map/all_to_all | solution.py:111
  148.3 0.6 copy.115
  148.9 0.8 copy.159
  149.7 0.8 copy.160
  (62 shorter events, 2.6 us)
Async XLA Ops:
  0.6 34.1 %copy-start = (bf16[1,2,8,512]{3,2,1,0:T(8,128)(2,1)S(1)}, bf16[1,2,8,512]{3,2,1,0:T(8,128)(2,1)}, u32[]{:S(2)}) copy-start(bf16[1,2,8,512]{3,2,1,0:T(8,128)(2,1)} %param.14) | copy-start | bytes 49156
  0.6 0.7 copy-start.16
  2.0 0.7 copy-start.17
  34.2 0.5 copy-start.14
  34.7 0.7 copy-start.1
  61.3 5.2 %copy-start.4 = (bf16[1,512,512]{2,1,0:T(8,128)(2,1)S(1)}, bf16[1,512,512]{2,1,0:T(8,128)(2,1)}, u32[]{:S(2)}) copy-start(bf16[1,512,512]{2,1,0:T(8,128)(2,1)} %param.12) | copy-start | bytes 1572868
  61.3 25.4 %all-to-all-start.2 = ((bf16[48,8,512]{2,1,0:T(8,128)(2,1)}), bf16[48,8,512]{2,1,0:T(8,128)(2,1)S(1)}, u32[]{:S(2)}, u32[]{:S(2)}) async-start(bf16[48,8,512]{2,1,0:T(8,128)(2,1)} %get-tuple-element.35), calls=%async_computation.2 | async-start | bytes 786432 | tf_op jit(solution)/shard_map/all_to_all | solution.py:85
  66.5 1.1 copy-start.2
  67.6 1.0 copy-start.3
  87.5 0.7 copy-start.8
  90.5 1.6 %copy-start.5 = (bf16[512,4,128]{2,1,0:T(4,128)(2,1)S(1)}, bf16[512,4,128]{2,1,0:T(4,128)(2,1)}, u32[]{:S(2)}) copy-start(bf16[512,4,128]{2,1,0:T(4,128)(2,1)} %reshape_squeeze.10) | copy-start | bytes 1572868
  92.1 1.5 copy-start.9
  93.6 1.5 %copy-start.18 = (f32[4,512]{1,0:T(4,128)}, f32[4,512]{1,0:T(4,128)S(1)}, u32[]{:S(2)}) copy-start(f32[4,512]{1,0:T(4,128)S(1)} %get-tuple-element.36) | copy-start | bytes 24580
  95.2 0.7 copy-start.12
  97.2 5.4 %copy-start.11 = (bf16[128,4,128]{2,1,0:T(4,128)(2,1)S(1)}, bf16[128,4,128]{2,1,0:T(4,128)(2,1)}, u32[]{:S(2)}) copy-start(bf16[128,4,128]{2,1,0:T(4,128)(2,1)} %reshape_reshape.12) | copy-start | bytes 393220
  97.2 5.4 %copy-start.20 = (f32[4,512]{1,0:T(4,128)S(1)}, f32[4,512]{1,0:T(4,128)}, u32[]{:S(2)}) copy-start(f32[4,512]{1,0:T(4,128)} %fusion.60) | copy-start | bytes 24580
  97.2 25.5 %all-to-all-start.4 = ((bf16[48,8,512]{2,1,0:T(8,128)(2,1)}), bf16[48,8,512]{2,1,0:T(8,128)(2,1)S(1)}, u32[]{:S(2)}, u32[]{:S(2)}) async-start(bf16[48,8,512]{2,1,0:T(8,128)(2,1)} %copy.113), calls=%async_computation.4 | async-start | bytes 786432 | tf_op jit(solution)/shard_map/all_to_all | solution.py:112
  105.6 2.4 %copy-start.7 = (bf16[128,4,128]{2,1,0:T(4,128)(2,1)S(1)}, bf16[128,4,128]{2,1,0:T(4,128)(2,1)}, u32[]{:S(2)}) copy-start(bf16[128,4,128]{2,1,0:T(4,128)(2,1)} %reshape_reshape.15) | copy-start | bytes 393220
  106.6 1.8 %copy-start.6 = (bf16[512,4,128]{2,1,0:T(4,128)(2,1)S(1)}, bf16[512,4,128]{2,1,0:T(4,128)(2,1)}, u32[]{:S(2)}) copy-start(bf16[512,4,128]{2,1,0:T(4,128)(2,1)} %reshape_squeeze.10) | copy-start | bytes 1572868
  106.6 27.5 %collective-permute-start = (bf16[1,512,512]{2,1,0:T(8,128)(2,1)}, bf16[1,512,512]{2,1,0:T(8,128)(2,1)S(1)}, u32[]{:S(2)}, u32[]{:S(2)}) collective-permute-start(bf16[1,512,512]{2,1,0:T(8,128)(2,1)} %add_convert_fusion.1), channel_id=1, source_target_pairs={{0,384},{1,385},{2,386},{3,387},{4,388},{5,389},{6,390},{7,391},{8... | collective-permute-start | bytes 1572872 | tf_op jit(solution)/shard_map/ppermute | solution.py:14
  110.7 0.7 copy-start.13
  112.7 15.3 %copy-start.10 = (bf16[128,4,128]{0,2,1:T(8,128)(2,1)S(1)}, bf16[128,4,128]{0,2,1:T(8,128)(2,1)}, u32[]{:S(2)}) copy-start(bf16[128,4,128]{0,2,1:T(8,128)(2,1)} %copy-done.9) | copy-start | bytes 393220
  112.7 15.3 %copy-start.19 = (f32[4,512]{1,0:T(4,128)S(1)}, f32[4,512]{1,0:T(4,128)}, u32[]{:S(2)}) copy-start(f32[4,512]{1,0:T(4,128)} %copy-done.18) | copy-start | bytes 24580
  122.7 25.3 %all-to-all-start.3 = ((bf16[48,8,512]{2,1,0:T(8,128)(2,1)}), bf16[48,8,512]{2,1,0:T(8,128)(2,1)S(1)}, u32[]{:S(2)}, u32[]{:S(2)}) async-start(bf16[48,8,512]{2,1,0:T(8,128)(2,1)} %copy.108), calls=%async_computation.3 | async-start | bytes 786432 | tf_op jit(solution)/shard_map/all_to_all | solution.py:111
  132.6 4.0 %copy-start.15 = (s32[48]{0:T(128)S(1)}, s32[48]{0:T(128)}, u32[]{:S(2)}) copy-start(s32[48]{0:T(128)} %copy-done.14) | copy-start | bytes 580
  132.8 3.8 %collective-permute-start.1 = (bf16[1,512,512]{2,1,0:T(8,128)(2,1)S(1)}, bf16[1,512,512]{2,1,0:T(8,128)(2,1)S(1)}, u32[]{:S(2)}, u32[]{:S(2)}) collective-permute-start(bf16[1,512,512]{2,1,0:T(8,128)(2,1)S(1)} %add_convert_fusion), channel_id=1, source_target_pairs={{384,0},{385,1},{386,2},{387,3},{388,4},{389,5},{390,6},{391,7},{3... | collective-permute-start | bytes 1572872 | tf_op jit(solution)/shard_map/ppermute | solution.py:14
where the time goes:
time: 151 us; the launch traced here: 150 us
  blocking collectives  54.6 us (36%)
  waiting for transfers between devices  39.8 us (26%)
  starting transfers between devices  18.6 us (12%)
  local copies, waits for them, and re-layouts  18.3 us (12%)
  matrix products  13.4 us (9%)
  other arithmetic  4.73 us (3%)
    all_to_all x1, blocking collectives, local(): lax.all_to_all(wanted.reshape(replicas, 1), 'dp', split_axis=0, concat_ax...  30.2 us
    all_to_all x1, blocking collectives, local(): lax.all_to_all(out_values, 'dp', split_axis=0, concat_axis=0, tiled=True)  24.4 us
    all_to_all x1, waiting for transfers between devices, local(): lax.all_to_all(out_keys, 'dp', split_axis=0, concat_axis=0, tiled=True)  16.7 us
    all_to_all x1, waiting for transfers between devices, local(): lax.all_to_all(send_keys, 'dp', split_axis=0, concat_axis=0, tiled=True)  10.6 us
    all_to_all x1, waiting for transfers between devices, local(): lax.all_to_all(send_values, 'dp', split_axis=0, concat_axis=0, tiled=True)  10 us
    unnamed x47, local copies, waits for them, and re-layouts  7.66 us
    all_to_all x1, starting transfers between devices, local(): lax.all_to_all(send_values, 'dp', split_axis=0, concat_axis=0, tiled=True)  5.37 us
    all_to_all x1, starting transfers between devices, local(): lax.all_to_all(send_keys, 'dp', split_axis=0, concat_axis=0, tiled=True)  5.24 us
  transfers between devices with their start and end apart: 5, of which 4 were waited for; matrix products, arithmetic and copies ran while one was open for 11% of the time, Pallas kernels for 0%

commit v1 on v0

v1 whole, which is shorter than its diff:
```python
import functools
import math

import jax
import jax.numpy as jnp
from jax import lax
from jax.experimental import pallas as pl
from jax.experimental.pallas import tpu as pltpu
from jax.sharding import PartitionSpec as P

HEAD = 128
X = 4
BF16 = jnp.bfloat16
F32 = jnp.float32
NT = (((1,), (1,)), ((), ()))
TN = (((0,), (0,)), ((), ()))


def wait_for(ref, sem):
    pltpu.make_async_copy(ref, ref, sem).wait()


def kernel(
    Z, blk, picks,
    stream_ref, saved_ref, grad_ref, mk_ref, mv_ref, om_ref, ids_ref,
    next_ref, back_ref, kg_ref, vg_ref,
    stream_v, saved_v, grad_v, mem_v, G, T, onehot, kb, vb, kf, vf, kt, vt, gs, res, zero,
    rkz, rvz, rva, rvb, rkx, om_s, ids_s,
    load_sem, small_sem, agk_x, agk_z, agv_z, agv_x, agv_r, ag_send,
    rsk_z, rsk_x, rsv_a, rsv_b, rsv_z, rs_send, pipe_send, pipe_recv, zero_sem,
):
    pipe, dp, ten = lax.axis_index("pipe"), lax.axis_index("dp"), lax.axis_index("tensor")
    z, x = dp // X, dp % X
    H = Z // 2
    W = stream_v.shape[1]
    heads = W // HEAD
    half = W // 2
    rows = 2 * blk
    scale = 1.0 / math.sqrt(HEAD)

    def at(dz, dx):
        return lax.rem(z + dz + Z, Z) * X + lax.rem(x + dx + X, X)

    def send(src, dst, ssem, rsem, dz, dx):
        pltpu.make_async_remote_copy(
            src_ref=src, dst_ref=dst, send_sem=ssem, recv_sem=rsem,
            device_id=(pipe, at(dz, dx), ten), device_id_type=pl.DeviceIdType.MESH,
        ).start()

    mem_loads = [
        pltpu.make_async_copy(mk_ref, mem_v.at[0], small_sem.at[0]),
        pltpu.make_async_copy(mv_ref, mem_v.at[1], small_sem.at[1]),
    ]
    id_loads = [
        pltpu.make_async_copy(om_ref, om_s, small_sem.at[2]),
        pltpu.make_async_copy(ids_ref, ids_s, small_sem.at[3]),
    ]
    loads = [
        pltpu.make_async_copy(saved_ref, saved_v, load_sem.at[0]),
        pltpu.make_async_copy(grad_ref, grad_v, load_sem.at[1]),
        pltpu.make_async_copy(stream_ref, stream_v, load_sem.at[2]),
    ]
    for copy in mem_loads + id_loads + loads:
        copy.start()

    barrier = pltpu.get_barrier_semaphore()
    for dz, dx in ((1, 0), (-1, 0), (0, 1), (0, 2), (0, 3)):
        pl.semaphore_signal(
            barrier, inc=1, device_id=(pipe, at(dz, dx), ten), device_id_type=pl.DeviceIdType.MESH
        )
    pl.semaphore_signal(
        barrier, inc=1, device_id=(1 - pipe, dp, ten), device_id_type=pl.DeviceIdType.MESH
    )
    for kv in range(2):
        mem_loads[kv].wait()
        own = jnp.concatenate([mem_v[kv, 0].astype(F32), mem_v[kv, 1].astype(F32)], axis=0)
        G[kv, dp] = own.astype(BF16)
    pl.semaphore_wait(barrier, 6)

    halves = (slice(0, half), slice(half, W))
    k_order = (0, 1, 3, 2)
    k_half = ((0, 1), (3, 2))

    def v_to_x(o):
        for d, dx in ((0, 1), (1, -1)):
            ref = G.at[1, at(o, 0)]
            send(ref, ref, ag_send.at[1], agv_x.at[d, o % Z], 0, dx)

    def v_relay(o):
        for d, dx in ((0, 1), (1, -1)):
            wait_for(G.at[1, at(o, -dx)], agv_x.at[d, o % Z])
            ref = G.at[1, at(o, -dx), :, halves[d]]
            send(ref, ref, ag_send.at[1], agv_r.at[d, o % Z], 0, dx)

    def v_relay_wait(o):
        for d in range(2):
            wait_for(G.at[1, at(o, 2), :, halves[d]], agv_r.at[d, o % Z])

    for r in (1, 3, 2):
        ref = G.at[0, dp]
        send(ref, ref, ag_send.at[0], agk_x.at[r - 1], 0, r)
    for d, dz in ((0, 1), (1, -1)):
        ref = G.at[1, dp]
        send(ref, ref, ag_send.at[1], agv_z.at[d, 0], dz, 0)
    v_to_x(0)
    for i, r in enumerate(k_order):
        if r:
            wait_for(G.at[0, at(0, r)], agk_x.at[(X - r) - 1])
        for d, dz in ((0, 1), (1, -1)):
            if H > 1 or r in k_half[d]:
                ref = G.at[0, at(0, r)]
                send(ref, ref, ag_send.at[0], agk_z.at[d, 0, r], dz, 0)

    for copy in id_loads:
        copy.wait()
    places = [[om_s[ids_s[m, 0, 0, j]] for j in range(picks)] for m in range(2)]
    total = Z * X * rows
    ramp = lax.broadcasted_iota(jnp.int32, (blk, total), 1) - lax.broadcasted_iota(
        jnp.int32, (blk, total), 0
    )
    for m in range(2):
        for j in range(0, picks, 2):
            pair = [
                jnp.where(ramp == places[m][i] * blk, 1.0, 0.0).astype(F32) for i in (j, j + 1)
            ]
            onehot[m, j * blk:(j + 2) * blk, :] = jnp.concatenate(pair, axis=0).astype(BF16)

    for s in range(1, H + 1):
        for d, dz in ((0, 1), (1, -1)):
            o = -dz * s
            if s < H:
                ref = G.at[1, at(o, 0)]
                wait_for(ref, agv_z.at[d, s - 1])
                if s + 1 < H:
                    send(ref, ref, ag_send.at[1], agv_z.at[d, s], dz, 0)
                else:
                    ref = G.at[1, at(o, 0), :, halves[d]]
                    send(ref, ref, ag_send.at[1], agv_z.at[d, s], dz, 0)
                v_to_x(o)
            else:
                wait_for(G.at[1, at(o, 0), :, halves[d]], agv_z.at[d, s - 1])
        if s == H:
            v_to_x(H)
        for o in ((0,) if s == 1 else (1 - s, s - 1)):
            v_relay(o)
        for r in k_order:
            for d, dz in ((0, 1), (1, -1)):
                if s == H and r not in k_half[d]:
                    continue
                ref = G.at[0, at(-dz * s, r)]
                wait_for(ref, agk_z.at[d, s - 1, r])
                if s + 1 < H or (s + 1 == H and r in k_half[d]):
                    send(ref, ref, ag_send.at[0], agk_z.at[d, s, r], dz, 0)
    v_relay(H)

    loads[0].wait()
    loads[1].wait()
    def select(m, kv):
        table = G[kv].reshape(total, W)
        return jnp.dot(onehot[m], table, preferred_element_type=F32).astype(BF16)

    kb[...] = select(1, 0)
    for o in range(Z):
        v_relay_wait(o)
    vb[...] = select(1, 1)

    def softmax_t(k_h, q_h):
        st = lax.dot_general(k_h, q_h, NT, preferred_element_type=F32) * scale
        e = jnp.exp(st - jnp.max(st, axis=0, keepdims=True))
        return e / jnp.sum(e, axis=0, keepdims=True)

    for h in range(heads):
        cut = slice(h * HEAD, (h + 1) * HEAD)
        q_h, g_h = saved_v[:, cut], grad_v[:, cut]
        w = softmax_t(kb[:, cut], q_h)
        gw = lax.dot_general(vb[:, cut], g_h, NT, preferred_element_type=F32)
        centre = jnp.sum(w * gw, axis=0, keepdims=True)
        gst = (w * (gw - centre) * scale).astype(BF16)
        gs[h] = gst
        kt[:, cut] = jnp.dot(gst, q_h, preferred_element_type=F32).astype(BF16)
        vt[:, cut] = jnp.dot(w.astype(BF16), g_h, preferred_element_type=F32).astype(BF16)

    lane = lax.broadcasted_iota(jnp.int32, (1, picks * blk), 1)
    target = lane % blk
    for j in range(picks):
        target = target + jnp.where(lane // blk == j, places[1][j] * blk, 0)
    spread = lax.broadcasted_iota(jnp.int32, (total, picks * blk), 0) == target
    spread = jnp.where(spread, 1.0, 0.0).astype(BF16)
    for kv, terms in ((0, kt), (1, vt)):
        T[kv] = jnp.dot(spread, terms[...], preferred_element_type=F32).astype(BF16).reshape(
            Z * X, rows, W
        )

    def k_start(s):
        for r in k_order:
            for d, dz in ((0, 1), (1, -1)):
                if (s == 1 and r not in k_half[d]) or (s == 2 and r in k_half[d]):
                    continue
                if s > 2:
                    continue
                send(
                    T.at[0, at(dz * (H + 1 - s), r)], rkz.at[d, s - 1, r], rs_send.at[0],
                    rsk_z.at[d, s - 1, r], dz, 0,
                )

    def k_step(s):
        for r in k_order:
            for d, dz in ((0, 1), (1, -1)):
                if s == 2 and r not in k_half[d]:
                    continue
                mine = rkz.at[d, s - 2, r]
                wait_for(mine, rsk_z.at[d, s - 2, r])
                mine[...] = (
                    mine[...].astype(F32) + T[0, at(dz * (H + 1 - s), r)].astype(F32)
                ).astype(BF16)
                send(mine, rkz.at[d, s - 1, r], rs_send.at[0], rsk_z.at[d, s - 1, r], dz, 0)

    def v_a(o):
        for d, dx in ((0, 1), (1, -1)):
            send(
                T.at[1, at(o, 2), :, halves[d]], rva.at[d, o % Z], rs_send.at[1],
                rsv_a.at[d, o % Z], 0, dx,
            )

    def v_b(o):
        for d, dx in ((0, 1), (1, -1)):
            wait_for(rva.at[d, o % Z], rsv_a.at[d, o % Z])
            part = T.at[1, at(o, dx), :, halves[d]]
            part[...] = (part[...].astype(F32) + rva[d, o % Z].astype(F32)).astype(BF16)
            send(
                T.at[1, at(o, dx)], rvb.at[d, o % Z], rs_send.at[1], rsv_b.at[d, o % Z], 0, dx
            )

    def v_c(o):
        for d in range(2):
            wait_for(rvb.at[d, o % Z], rsv_b.at[d, o % Z])
        mine = T.at[1, at(o, 0)]
        mine[...] = (
            mine[...].astype(F32) + rvb[0, o % Z].astype(F32) + rvb[1, o % Z].astype(F32)
        ).astype(BF16)

    def v_z(s):
        for d, dz in ((0, 1), (1, -1)):
            o = dz * (H + 1 - s)
            if s == 1:
                send(
                    T.at[1, at(o, 0), :, halves[d]], rvz.at[d, 0, :, halves[d]], rs_send.at[1],
                    rsv_z.at[d, 0], dz, 0,
                )
                continue
            mine = T.at[1, at(o, 0)]
            if s == 2:
                got = rvz.at[d, 0, :, halves[d]]
                mine = T.at[1, at(o, 0), :, halves[d]]
            else:
                got = rvz.at[d, s - 2]
            wait_for(got, rsv_z.at[d, s - 2])
            mine[...] = (mine[...].astype(F32) + got[...].astype(F32)).astype(BF16)
            send(T.at[1, at(o, 0)], rvz.at[d, s - 1], rs_send.at[1], rsv_z.at[d, s - 1], dz, 0)

    def pair(i):
        return (i,) if i in (0, H) else (i, -i)

    def other_head(h):
        cut = slice(h * HEAD, (h + 1) * HEAD)

        @pl.when(pipe == 0)
        def _():
            s_h = stream_v[:, cut]
            w = softmax_t(kf[:, cut], s_h).astype(BF16)
            out = lax.dot_general(w, vf[:, cut], TN, preferred_element_type=F32)
            res[:, cut] = (s_h.astype(F32) + out).astype(BF16)

        @pl.when(pipe == 1)
        def _():
            out = lax.dot_general(gs[h], kb[:, cut], TN, preferred_element_type=F32)
            res[:, cut] = (grad_v[:, cut].astype(F32) + out).astype(BF16)

    def exchange(out_ref):
        return pltpu.make_async_remote_copy(
            src_ref=res, dst_ref=out_ref, send_sem=pipe_send, recv_sem=pipe_recv,
            device_id=(1 - pipe, dp, ten), device_id_type=pl.DeviceIdType.MESH,
        )

    def blank(out_ref):
        return pltpu.make_async_copy(zero, out_ref, zero_sem)

    k_start(1)
    for i in range(H, -1, -1):
        for o in pair(i):
            v_a(o)
        if i == H:
            k_start(2)
    zero[...] = jnp.zeros_like(zero)

    @pl.when(pipe == 0)
    def _():
        blank(next_ref).start()

    @pl.when(pipe == 1)
    def _():
        blank(back_ref).start()

    for o in pair(H) + pair(H - 1):
        v_b(o)
    loads[2].wait()

    @pl.when(pipe == 0)
    def _():
        kf[...] = select(0, 0)
        vf[...] = select(0, 1)

    done = 0
    for s in range(1, H + 1):
        if s >= 2:
            k_step(s)
        if H - 1 - s >= 0:
            for o in pair(H - 1 - s):
                v_b(o)
        for o in pair(H + 1 - s):
            v_c(o)
        v_z(s)
        if done < heads:
            other_head(done)
            done += 1
        if done == heads:
            done += 1

            @pl.when(pipe == 0)
            def _():
                exchange(next_ref).start()

            @pl.when(pipe == 1)
            def _():
                exchange(back_ref).start()

    last = []
    for r in k_order:
        mine = T.at[0, at(0, r)]
        total_r = mine[...].astype(F32)
        for d in range(2):
            got = rkz.at[d, H - 1, r]
            wait_for(got, rsk_z.at[d, H - 1, r])
            total_r = total_r + got[...].astype(F32)
        if r == 0:
            key_total = total_r
        else:
            mine[...] = total_r.astype(BF16)
            send(mine, rkx.at[r - 1], rs_send.at[0], rsk_x.at[r - 1], 0, r)
    v_c(0)
    value_total = T[1, dp].astype(F32)
    for d in range(2):
        got = rvz.at[d, H - 1]
        wait_for(got, rsv_z.at[d, H - 1])
        value_total = value_total + got[...].astype(F32)
    for i in range(2):
        vg_ref[i] = value_total[i * blk:(i + 1) * blk].astype(BF16)
    for r in (1, 3, 2):
        wait_for(rkx.at[r - 1], rsk_x.at[r - 1])
        key_total = key_total + rkx[r - 1].astype(F32)
    for i in range(2):
        kg_ref[i] = key_total[i * blk:(i + 1) * blk].astype(BF16)

    sent = Z * X - 1
    for kv in range(2):
        wait_for(G.at[kv, 0:sent], ag_send.at[kv])
        wait_for(T.at[kv, 0:sent], rs_send.at[kv])
    wait_for(res, pipe_send)
    wait_for(res, pipe_recv)
    wait_for(zero, zero_sem)


def local(stream_in, saved_in, grad_out, mem_keys, mem_values, owner_map, block_ids):
    Z = lax.axis_size("dp") // X
    H = Z // 2
    n_blk, blk = mem_keys.shape[1:3]
    picks = block_ids.shape[3]
    tokens, W = stream_in.shape[1:]
    heads = W // HEAD
    rows = n_blk * blk
    got = picks * blk
    DMA = pltpu.SemaphoreType.DMA
    anywhere = pl.BlockSpec(memory_space=pl.ANY)
    outs = pl.pallas_call(
        functools.partial(kernel, Z, blk, picks),
        out_shape=(
            jax.ShapeDtypeStruct((tokens, W), BF16),
            jax.ShapeDtypeStruct((tokens, W), BF16),
            jax.ShapeDtypeStruct((n_blk, blk, W), BF16),
            jax.ShapeDtypeStruct((n_blk, blk, W), BF16),
        ),
        in_specs=[anywhere] * 7,
        out_specs=(
            anywhere, anywhere,
            pl.BlockSpec(memory_space=pltpu.VMEM), pl.BlockSpec(memory_space=pltpu.VMEM),
        ),
        scratch_shapes=[
            pltpu.VMEM((tokens, W), BF16),
            pltpu.VMEM((tokens, W), BF16),
            pltpu.VMEM((tokens, W), BF16),
            pltpu.VMEM((2, n_blk, blk, W), BF16),
            pltpu.VMEM((2, Z * X, rows, W), BF16),
            pltpu.VMEM((2, Z * X, rows, W), BF16),
            pltpu.VMEM((2, got, Z * X * rows), BF16),
            pltpu.VMEM((got, W), BF16),
            pltpu.VMEM((got, W), BF16),
            pltpu.VMEM((got, W), BF16),
            pltpu.VMEM((got, W), BF16),
            pltpu.VMEM((got, W), BF16),
            pltpu.VMEM((got, W), BF16),
            pltpu.VMEM((heads, got, tokens), BF16),
            pltpu.VMEM((tokens, W), BF16),
            pltpu.VMEM((tokens, W), BF16),
            pltpu.VMEM((2, H, X, rows, W), BF16),
            pltpu.VMEM((2, H, rows, W), BF16),
            pltpu.VMEM((2, Z, rows, W // 2), BF16),
            pltpu.VMEM((2, Z, rows, W), BF16),
            pltpu.VMEM((X - 1, rows, W), BF16),
            pltpu.SMEM(owner_map.shape, jnp.int32),
            pltpu.SMEM(block_ids.shape, jnp.int32),
            DMA((3,)), DMA((4,)),
            DMA((X - 1,)), DMA((2, H, X)), DMA((2, H)), DMA((2, Z)), DMA((2, Z)), DMA((2,)),
            DMA((2, H, X)), DMA((X - 1,)), DMA((2, Z)), DMA((2, Z)), DMA((2, H)), DMA((2,)),
            DMA(()), DMA(()), DMA(()),
        ],
        compiler_params=pltpu.CompilerParams(
            collective_id=0, has_side_effects=True, vmem_limit_bytes=40 << 20
        ),
    )(
        stream_in[0], saved_in[0], grad_out[0], mem_keys[0], mem_values[0], owner_map, block_ids
    )
    return tuple(out[None] for out in outs)


def solution(mesh):
    in_specs = (
        P("pipe", "dp", "tensor"),
        P("pipe", "dp", "tensor"),
        P("pipe", "dp", "tensor"),
        P("pipe", "dp", None, "tensor"),
        P("pipe", "dp", None, "tensor"),
        P(),
        P(None, "pipe", "dp", None),
    )
    out_specs = (
        P("pipe", "dp", "tensor"),
        P("pipe", "dp", "tensor"),
        P("pipe", "dp", None, "tensor"),
        P("pipe", "dp", None, "tensor"),
    )
    return jax.shard_map(local, mesh=mesh, in_specs=in_specs, out_specs=out_specs, check_vma=False)
```

time: 151 us -> 83 us (0.55)
  Pallas kernels: 0 us -> 73.9 us
  blocking collectives: 54.6 us -> 0 us
  waiting for transfers between devices: 39.8 us -> 0 us
  starting transfers between devices: 18.6 us -> 0 us
  matrix products: 13.4 us -> 0 us
  local copies, waits for them, and re-layouts: 18.3 us -> 8.02 us
  other arithmetic: 4.73 us -> 0 us
    pallas_call x0 -> x1, Pallas kernels: none -> 73.9 us  [local(): pl.pallas_call(functools.partial(kernel, Z, blk, picks), out_shape=(jax.S...]
    all_to_all x2 -> x0, blocking collectives: 54.6 us -> none  [the longest x1 30.2 us: local(): lax.all_to_all(wanted.reshape(replicas, 1), 'dp', split_axis=0, concat_ax...]
    all_to_all x3 -> x0, waiting for transfers between devices: 37.3 us -> none  [the longest x1 16.7 us: local(): lax.all_to_all(out_keys, 'dp', split_axis=0, concat_axis=0, tiled=True)]
    all_to_all x3 -> x0, starting transfers between devices: 15.8 us -> none  [the longest x1 5.37 us: local(): lax.all_to_all(send_values, 'dp', split_axis=0, concat_axis=0, tiled=True)]
    dot_general x10 -> x0, matrix products: 10.9 us -> none  [the longest x1 3.1 us: backward_part(): jnp.einsum('htk,khd->thd', grad_scores, key_rows, preferred_element_type=...]
    reshape x2 -> x0, local copies, waits for them, and re-layouts: 3.11 us -> none  [the longest x1 1.55 us: forward_part(): attended = jnp.einsum('htk,khd->thd', rounded, value_rows, preferred_elem...]
    another operation x8 -> x0, local copies, waits for them, and re-layouts: 2.74 us -> none  [the longest x2 1.37 us: forward_part(): value_rows = memory_values.reshape(-1, heads_count, HEAD_DIM)]
    ppermute x2 -> x0, starting transfers between devices: 2.73 us -> none  [from_behind(): return lax.ppermute(x, axis, pairs)]
  transfers between devices with their start and end apart: 5 -> 0, of which waited for: 4 -> 0; matrix products, arithmetic and copies ran while one was open for 11% -> 0% of each run, Pallas kernels for 0% -> 0%
where the time goes in v1:
time: 83 us; the launch traced here: 82.6 us
  Pallas kernels  73.9 us (89%)
  local copies, waits for them, and re-layouts  8.02 us (10%)
    pallas_call x1, Pallas kernels, local(): pl.pallas_call(functools.partial(kernel, Z, blk, picks), out_shape=(jax.S...  73.9 us
    unnamed x18, local copies, waits for them, and re-layouts  8.02 us

profile of v1, /device:TPU:56, one launch (start us, length us, event | category | flops | bytes accessed | tf_op | source)
XLA Modules:
  0.0 82.6 jit_solution(6973732477860915694)
XLA Ops:
  0.6 0.0 copy-start.5
  0.6 0.0 copy-start.6
  0.7 0.7 copy-done.5
  1.3 0.0 copy-done.6
  1.3 0.0 copy-start
  1.3 1.0 %copy-done = bf16[1,512,512]{2,1,0:T(8,128)(2,1)S(1)} copy-done((bf16[1,512,512]{2,1,0:T(8,128)(2,1)S(1)}, bf16[1,512,512]{2,1,0:T(8,128)(2,1)}, u32[]{:S(2)}) %copy-start) | copy-done | bytes 524312
  2.4 0.0 copy-start.1
  2.4 1.0 %copy-done.1 = bf16[1,512,512]{2,1,0:T(8,128)(2,1)S(1)} copy-done((bf16[1,512,512]{2,1,0:T(8,128)(2,1)S(1)}, bf16[1,512,512]{2,1,0:T(8,128)(2,1)}, u32[]{:S(2)}) %copy-start.1) | copy-done | bytes 524312
  3.4 0.0 copy-start.2
  3.4 1.0 %copy-done.2 = bf16[1,512,512]{2,1,0:T(8,128)(2,1)S(1)} copy-done((bf16[1,512,512]{2,1,0:T(8,128)(2,1)S(1)}, bf16[1,512,512]{2,1,0:T(8,128)(2,1)}, u32[]{:S(2)}) %copy-start.2) | copy-done | bytes 524312
  4.4 0.0 copy-start.3
  4.4 0.7 copy-done.3
  5.2 0.0 copy-start.4
  5.2 0.7 copy-done.4
  5.9 73.9 %shard_map.102 = (bf16[512,512]{1,0:T(8,128)(2,1)S(1)}, bf16[512,512]{1,0:T(8,128)(2,1)S(1)}, bf16[2,8,512]{2,1,0:T(8,128)(2,1)S(1)}, bf16[2,8,512]{2,1,0:T(8,128)(2,1)S(1)}) custom-call(bf16[512,512]{1,0:T(8,128)(2,1)S(1)} %bitcast.9, bf16[512,512]{1,0:T(8,128)(2,1)S(1)} %bitcast.10, bf16[512,512]{1,0:T(8,128)(2,1)S(1)} %bitcast.11, ...), custom_call_target="tpu_custom_call" | custom-call | tf_op jit(solution)/shard_map/pallas_call | solution.py:384
  79.8 0.8 copy.15
  80.6 0.8 copy.16
  81.4 0.6 copy.17
  82.0 0.6 copy.18
Async XLA Ops:
  0.6 0.7 copy-start.5
  0.6 0.7 copy-start.6
  1.3 1.0 %copy-start = (bf16[1,512,512]{2,1,0:T(8,128)(2,1)S(1)}, bf16[1,512,512]{2,1,0:T(8,128)(2,1)}, u32[]{:S(2)}) copy-start(bf16[1,512,512]{2,1,0:T(8,128)(2,1)} %param.7) | copy-start | bytes 1572868
  2.4 1.0 %copy-start.1 = (bf16[1,512,512]{2,1,0:T(8,128)(2,1)S(1)}, bf16[1,512,512]{2,1,0:T(8,128)(2,1)}, u32[]{:S(2)}) copy-start(bf16[1,512,512]{2,1,0:T(8,128)(2,1)} %param.8) | copy-start | bytes 1572868
  3.4 1.0 %copy-start.2 = (bf16[1,512,512]{2,1,0:T(8,128)(2,1)S(1)}, bf16[1,512,512]{2,1,0:T(8,128)(2,1)}, u32[]{:S(2)}) copy-start(bf16[1,512,512]{2,1,0:T(8,128)(2,1)} %param.9) | copy-start | bytes 1572868
  4.4 0.7 copy-start.3
  5.2 0.7 copy-start.4

commit v2 on v0

v2 whole, which is shorter than its diff:
```python
import functools
import math

import jax
import jax.numpy as jnp
from jax import lax
from jax.experimental import pallas as pl
from jax.experimental.pallas import tpu as pltpu
from jax.sharding import PartitionSpec as P

HEAD = 128
X = 4
Z = 12
LANES = 128
BF16 = jnp.bfloat16
F32 = jnp.float32
NT = (((1,), (1,)), ((), ()))
TN = (((0,), (0,)), ((), ()))
MESH = pl.DeviceIdType.MESH
SIDES = ((0, 1), (1, -1))
FAR = (6, 5, -5, 4, -4)
VMEM_LIMIT = 60 << 20


def wait_for(ref, sem):
    pltpu.make_async_copy(ref, ref, sem).wait()


def main_kernel(
    blk, picks,
    stream_ref, saved_ref, grad_ref, mk_ref, mv_ref, om_ref, ids_ref,
    recv_ref, kg_ref, vg_ref,
    stream_v, saved_v, grad_v, mem_v, tab, G, S, C, pick, spread, kvb, kvf, terms, gs, res,
    T, rx, U, rr, rf, om_s, ids_s, tab_s,
    load_sem, small_sem, tab_send, tab_recv, tab_sem, agz, agx, agz_send, agx_send,
    rsx, rsr, rsf, rsx_send, rsz_send, pipe_send, pipe_recv,
):
    pipe, dp, ten = lax.axis_index("pipe"), lax.axis_index("dp"), lax.axis_index("tensor")
    z, x = dp // X, dp % X
    W = stream_v.shape[1]
    heads = W // HEAD
    keys = picks * blk
    both = 2 * blk
    total = Z * X * both
    scale = 1.0 / math.sqrt(HEAD)

    def zat(dz):
        return lax.rem(z + dz + Z, Z)

    def at(dz, dx):
        return zat(dz) * X + lax.rem(x + dx + X, X)

    def send(src, dst, ssem, rsem, dz, dx):
        pltpu.make_async_remote_copy(
            src_ref=src, dst_ref=dst, send_sem=ssem, recv_sem=rsem,
            device_id=(pipe, at(dz, dx), ten), device_id_type=MESH,
        ).start()

    mem_loads = [
        pltpu.make_async_copy(mk_ref, mem_v.at[0], small_sem.at[0]),
        pltpu.make_async_copy(mv_ref, mem_v.at[1], small_sem.at[1]),
    ]
    id_loads = [
        pltpu.make_async_copy(om_ref, om_s, small_sem.at[2]),
        pltpu.make_async_copy(ids_ref, ids_s, small_sem.at[3]),
    ]
    loads = [
        pltpu.make_async_copy(saved_ref, saved_v, load_sem.at[0]),
        pltpu.make_async_copy(grad_ref, grad_v, load_sem.at[1]),
        pltpu.make_async_copy(stream_ref, stream_v, load_sem.at[2]),
    ]
    for copy in mem_loads + id_loads:
        copy.start()
    barrier = pltpu.get_barrier_semaphore()
    partners = [(dz, 0) for dz in (3, -3, 2, -2, 1, -1)] + [(0, dx) for dx in range(1, X)]
    for dz, dx in partners:
        pl.semaphore_signal(
            barrier, inc=1, device_id=(pipe, at(dz, dx), ten), device_id_type=MESH
        )
    pl.semaphore_signal(barrier, inc=1, device_id=(1 - pipe, dp, ten), device_id_type=MESH)
    for copy in loads:
        copy.start()

    for copy in id_loads:
        copy.wait()
    places = [[om_s[ids_s[m, 0, 0, j]] for j in range(picks)] for m in range(2)]
    owners = [[place // 2 for place in row] for row in places]
    lane = lax.broadcasted_iota(jnp.int32, (8, LANES), 1)
    wanted = jnp.zeros((8, LANES), jnp.int32)
    for m in range(2):
        for j in range(picks):
            wanted = jnp.where(lane == owners[m][j], places[m][j] % 2, wanted)
    tab[0] = wanted
    for copy in mem_loads:
        copy.wait()
    for i in range(2):
        own = jnp.concatenate([mem_v[0, i].astype(F32), mem_v[1, i].astype(F32)], axis=0)
        G[z, i] = own.astype(BF16)
    pl.semaphore_wait(barrier, len(partners) + 1)

    for dz in (3, -3, 2, -2, 1, -1):
        send(G.at[z], G.at[z], agz_send, agz.at[(-dz) % Z], dz, 0)
    for dx in range(1, X):
        send(tab.at[0], tab.at[X - dx], tab_send, tab_recv.at[X - dx - 1], 0, dx)

    ramp = lax.broadcasted_iota(jnp.int32, (blk, total), 1) - lax.broadcasted_iota(
        jnp.int32, (blk, total), 0
    )
    for m in (1, 0):
        for kv in range(2):
            for j in range(0, picks, 2):
                pair = [
                    jnp.where(ramp == owners[m][i] * both + kv * blk, 1.0, 0.0).astype(F32)
                    for i in (j, j + 1)
                ]
                row = kv * keys + j * blk
                pick[m, row:row + both, :] = jnp.concatenate(pair, axis=0).astype(BF16)

    for dx in range(1, X):
        wait_for(tab.at[dx], tab_recv.at[dx - 1])
    to_scalars = pltpu.make_async_copy(tab, tab_s, tab_sem)
    to_scalars.start()
    for d, sg in SIDES:
        far = G.at[zat(-3 * sg)]
        wait_for(far, agz.at[(-3 * sg) % Z])
        send(far, far, agz_send, agz.at[(-4 * sg) % Z], sg, 0)
        send(far, far, agz_send, agz.at[(-5 * sg) % Z], 2 * sg, 0)
        part = G.at[zat(-3 * sg), d]
        send(part, part, agz_send, agz.at[6 + d * Z], 3 * sg, 0)
    to_scalars.wait()

    def slot(dx, o):
        return tab_s[dx, 0, at(o, 0)]

    for o in (0, 3, -3, 1, -1, 2, -2, 4, -4, 5, -5, 6):
        if o == 6:
            for d, _ in SIDES:
                wait_for(G.at[zat(6), d], agz.at[6 + d * Z])
        elif abs(o) not in (0, 3):
            wait_for(G.at[zat(o)], agz.at[o % Z])
        first, second = G[zat(o), 0], G[zat(o), 1]
        for dx in (2, 1, 3):
            S[dx - 1, o % Z] = jnp.where(slot(dx, o) == 1, second, first)
            send(
                S.at[dx - 1, o % Z], C.at[at(o, 0)], agx_send, agx.at[X - dx - 1, o % Z], 0, dx
            )
        C[at(o, 0)] = jnp.where(slot(0, o) == 1, second, first)

    column = lax.broadcasted_iota(jnp.int32, (1, 2 * keys), 1)
    target = column % blk + jnp.where(column >= keys, blk, 0)
    for j in range(picks):
        target = target + jnp.where((column % keys) // blk == j, owners[1][j] * both, 0)
    hits = lax.broadcasted_iota(jnp.int32, (total, 2 * keys), 0) == target
    spread[...] = jnp.where(hits, 1.0, 0.0).astype(BF16)

    for copy in loads:
        copy.wait()
    for o in (0, 3, -3, 1, -1, 2, -2, 4, -4, 5, -5, 6):
        for dx in range(1, X):
            wait_for(C.at[at(o, dx)], agx.at[dx - 1, o % Z])

    def select(m):
        return jnp.dot(
            pick[m], C[...].reshape(total, W), preferred_element_type=F32
        ).astype(BF16)

    def softmax_t(k_h, q_h):
        st = lax.dot_general(k_h, q_h, NT, preferred_element_type=F32) * scale
        e = jnp.exp(st - jnp.max(st, axis=0, keepdims=True))
        return e * (1.0 / jnp.sum(e, axis=0, keepdims=True))

    kvb[...] = select(1)
    for h in range(heads):
        cut = slice(h * HEAD, (h + 1) * HEAD)
        q_h, g_h = saved_v[:, cut], grad_v[:, cut]
        w = softmax_t(kvb[0:keys, cut], q_h)
        gw = lax.dot_general(kvb[keys:, cut], g_h, NT, preferred_element_type=F32)
        centre = jnp.sum(w * gw, axis=0, keepdims=True)
        gst = (w * (gw - centre) * scale).astype(BF16)
        gs[h] = gst
        terms[0:keys, cut] = jnp.dot(gst, q_h, preferred_element_type=F32).astype(BF16)
        terms[keys:, cut] = jnp.dot(
            w.astype(BF16), g_h, preferred_element_type=F32
        ).astype(BF16)
    T[...] = jnp.dot(spread[...], terms[...], preferred_element_type=F32).astype(BF16).reshape(
        Z * X, both, W
    )

    for o in FAR + (3, -3, 2, -2, 1, -1, 0):
        for dx in (2, 1, 3):
            send(T.at[at(o, dx)], rx.at[X - dx - 1, o % Z], rsx_send, rsx.at[X - dx - 1, o % Z], 0, dx)

    def exchange():
        return pltpu.make_async_remote_copy(
            src_ref=res, dst_ref=recv_ref, send_sem=pipe_send, recv_sem=pipe_recv,
            device_id=(1 - pipe, dp, ten), device_id_type=MESH,
        )

    @pl.when(pipe == 0)
    def _():
        kvf[...] = select(0)
        for h in range(heads):
            cut = slice(h * HEAD, (h + 1) * HEAD)
            s_h = stream_v[:, cut]
            w = softmax_t(kvf[0:keys, cut], s_h).astype(BF16)
            out = lax.dot_general(w, kvf[keys:, cut], TN, preferred_element_type=F32)
            res[:, cut] = (s_h.astype(F32) + out).astype(BF16)

    @pl.when(pipe == 1)
    def _():
        for h in range(heads):
            cut = slice(h * HEAD, (h + 1) * HEAD)
            out = lax.dot_general(gs[h], kvb[0:keys, cut], TN, preferred_element_type=F32)
            res[:, cut] = (grad_v[:, cut].astype(F32) + out).astype(BF16)

    exchange().start()

    def combine(o):
        for dx in range(1, X):
            wait_for(rx.at[dx - 1, o % Z], rsx.at[dx - 1, o % Z])
        sums = [None, None]
        for dx in range(X):
            part = (T[at(o, 0)] if dx == 0 else rx[dx - 1, o % Z]).astype(F32)
            second = slot(dx, o).astype(F32)
            for i, share in enumerate((1.0 - second, second)):
                sums[i] = part * share if sums[i] is None else sums[i] + part * share
        return sums

    def keep(o):
        for i, value in enumerate(combine(o)):
            U[o % Z, i] = value.astype(BF16)

    def relay(d, sg):
        mine = [U[(3 * sg) % Z, i].astype(F32) for i in range(2)]
        for k in range(2):
            wait_for(rr.at[d, k], rsr.at[d, k])
            mine = [mine[i] + rr[d, k, i].astype(F32) for i in range(2)]
        wait_for(rr.at[d, 2, d], rsr.at[d, 2])
        mine[d] = mine[d] + rr[d, 2, d].astype(F32)
        for i in range(2):
            U[(3 * sg) % Z, i] = mine[i].astype(BF16)
        send(U.at[(3 * sg) % Z], rf.at[d, 2], rsz_send, rsf.at[d, 2], 3 * sg, 0)

    keep(6)
    for d, sg in SIDES:
        send(U.at[6, d], rr.at[d, 2, d], rsz_send, rsr.at[d, 2], 3 * sg, 0)
    for k in (1, 0):
        for d, sg in SIDES:
            o = sg * (4 + k)
            keep(o)
            send(U.at[o % Z], rr.at[d, k], rsz_send, rsr.at[d, k], sg * (k + 1), 0)
    for d, sg in SIDES:
        keep(3 * sg)
    for d, sg in SIDES:
        keep(2 * sg)
        send(U.at[(2 * sg) % Z], rf.at[d, 1], rsz_send, rsf.at[d, 1], 2 * sg, 0)
    for d, sg in SIDES:
        relay(d, sg)
    for d, sg in SIDES:
        keep(sg)
        send(U.at[sg % Z], rf.at[d, 0], rsz_send, rsf.at[d, 0], sg, 0)
    last = combine(0)
    for k in range(3):
        for d, sg in SIDES:
            wait_for(rf.at[d, k], rsf.at[d, k])
            last = [last[i] + rf[d, k, i].astype(F32) for i in range(2)]
    for i in range(2):
        kg_ref[i] = last[i][0:blk].astype(BF16)
        vg_ref[i] = last[i][blk:].astype(BF16)

    wait_for(tab.at[0:X - 1], tab_send)
    wait_for(G.at[0:Z - 1], agz_send)
    wait_for(U.at[0:Z - 1], rsz_send)
    wait_for(C.at[0:(X - 1) * Z], agx_send)
    wait_for(T.at[0:(X - 1) * Z], rsx_send)
    wait_for(res, pipe_send)
    wait_for(res, pipe_recv)


def write_kernel(recv_ref, kg_ref, vg_ref, next_ref, back_ref, kgo_ref, vgo_ref, zero, sem):
    pipe = lax.axis_index("pipe")
    copies = [
        pltpu.make_async_copy(kg_ref, kgo_ref, sem.at[0]),
        pltpu.make_async_copy(vg_ref, vgo_ref, sem.at[1]),
    ]
    for copy in copies:
        copy.start()

    def finish(got_ref, blank_ref):
        got = pltpu.make_async_copy(recv_ref, got_ref, sem.at[2])
        got.start()
        zero[...] = jnp.zeros_like(zero)
        blank = pltpu.make_async_copy(zero, blank_ref, sem.at[3])
        blank.start()
        got.wait()
        blank.wait()

    @pl.when(pipe == 0)
    def _():
        finish(back_ref, next_ref)

    @pl.when(pipe == 1)
    def _():
        finish(next_ref, back_ref)

    for copy in copies:
        copy.wait()


def local(stream_in, saved_in, grad_out, mem_keys, mem_values, owner_map, block_ids):
    n_blk, blk = mem_keys.shape[1:3]
    picks = block_ids.shape[3]
    tokens, W = stream_in.shape[1:]
    heads = W // HEAD
    keys = picks * blk
    both = 2 * blk
    DMA = pltpu.SemaphoreType.DMA
    anywhere = pl.BlockSpec(memory_space=pl.ANY)
    in_vmem = pl.BlockSpec(memory_space=pltpu.VMEM)
    wide = jax.ShapeDtypeStruct((tokens, W), BF16)
    small = jax.ShapeDtypeStruct((n_blk, blk, W), BF16)
    recv, kg, vg = pl.pallas_call(
        functools.partial(main_kernel, blk, picks),
        out_shape=(wide, small, small),
        in_specs=[anywhere] * 7,
        out_specs=(anywhere, in_vmem, in_vmem),
        scratch_shapes=[
            pltpu.VMEM((tokens, W), BF16),
            pltpu.VMEM((tokens, W), BF16),
            pltpu.VMEM((tokens, W), BF16),
            pltpu.VMEM((2, n_blk, blk, W), BF16),
            pltpu.VMEM((X, 8, LANES), jnp.int32),
            pltpu.VMEM((Z, 2, both, W), BF16),
            pltpu.VMEM((X - 1, Z, both, W), BF16),
            pltpu.VMEM((Z * X, both, W), BF16),
            pltpu.VMEM((2, 2 * keys, Z * X * both), BF16),
            pltpu.VMEM((Z * X * both, 2 * keys), BF16),
            pltpu.VMEM((2 * keys, W), BF16),
            pltpu.VMEM((2 * keys, W), BF16),
            pltpu.VMEM((2 * keys, W), BF16),
            pltpu.VMEM((heads, keys, tokens), BF16),
            pltpu.VMEM((tokens, W), BF16),
            pltpu.VMEM((Z * X, both, W), BF16),
            pltpu.VMEM((X - 1, Z, both, W), BF16),
            pltpu.VMEM((Z, 2, both, W), BF16),
            pltpu.VMEM((2, 3, 2, both, W), BF16),
            pltpu.VMEM((2, 3, 2, both, W), BF16),
            pltpu.SMEM(owner_map.shape, jnp.int32),
            pltpu.SMEM(block_ids.shape, jnp.int32),
            pltpu.SMEM((X, 8, LANES), jnp.int32),
            DMA((3,)), DMA((4,)), DMA(()), DMA((X - 1,)), DMA(()),
            DMA((2 * Z,)), DMA((X - 1, Z)), DMA(()), DMA(()),
            DMA((X - 1, Z)), DMA((2, 3)), DMA((2, 3)), DMA(()), DMA(()), DMA(()), DMA(()),
        ],
        compiler_params=pltpu.CompilerParams(
            collective_id=0, has_side_effects=True, vmem_limit_bytes=VMEM_LIMIT
        ),
    )(
        stream_in[0], saved_in[0], grad_out[0], mem_keys[0], mem_values[0], owner_map, block_ids
    )
    outs = pl.pallas_call(
        write_kernel,
        out_shape=(wide, wide, small, small),
        in_specs=[anywhere] * 3,
        out_specs=(anywhere,) * 4,
        scratch_shapes=[pltpu.VMEM((tokens, W), BF16), DMA((4,))],
        compiler_params=pltpu.CompilerParams(vmem_limit_bytes=VMEM_LIMIT),
    )(recv, kg, vg)
    return tuple(out[None] for out in outs)


def solution(mesh):
    in_specs = (
        P("pipe", "dp", "tensor"),
        P("pipe", "dp", "tensor"),
        P("pipe", "dp", "tensor"),
        P("pipe", "dp", None, "tensor"),
        P("pipe", "dp", None, "tensor"),
        P(),
        P(None, "pipe", "dp", None),
    )
    out_specs = (
        P("pipe", "dp", "tensor"),
        P("pipe", "dp", "tensor"),
        P("pipe", "dp", None, "tensor"),
        P("pipe", "dp", None, "tensor"),
    )
    return jax.shard_map(local, mesh=mesh, in_specs=in_specs, out_specs=out_specs, check_vma=False)
```

time: 151 us -> 67.9 us (0.45)
  Pallas kernels: 0 us -> 66.9 us
  blocking collectives: 54.6 us -> 0 us
  waiting for transfers between devices: 39.8 us -> 0 us
  starting transfers between devices: 18.6 us -> 0 us
  local copies, waits for them, and re-layouts: 18.3 us -> 0 us
  matrix products: 13.4 us -> 0 us
  other arithmetic: 4.73 us -> 0 us
    pallas_call x0 -> x2, Pallas kernels: none -> 66.9 us  [the longest x1 48.9 us: local(): pl.pallas_call(functools.partial(main_kernel, blk, picks), out_shape=(wid...]
    all_to_all x2 -> x0, blocking collectives: 54.6 us -> none  [the longest x1 30.2 us: local(): lax.all_to_all(wanted.reshape(replicas, 1), 'dp', split_axis=0, concat_ax...]
    all_to_all x3 -> x0, waiting for transfers between devices: 37.3 us -> none  [the longest x1 16.7 us: local(): lax.all_to_all(out_keys, 'dp', split_axis=0, concat_axis=0, tiled=True)]
    all_to_all x3 -> x0, starting transfers between devices: 15.8 us -> none  [the longest x1 5.37 us: local(): lax.all_to_all(send_values, 'dp', split_axis=0, concat_axis=0, tiled=True)]
    dot_general x10 -> x0, matrix products: 10.9 us -> none  [the longest x1 3.1 us: backward_part(): jnp.einsum('htk,khd->thd', grad_scores, key_rows, preferred_element_type=...]
    unnamed x47 -> x0, local copies, waits for them, and re-layouts: 7.66 us -> none
    reshape x2 -> x0, local copies, waits for them, and re-layouts: 3.11 us -> none  [the longest x1 1.55 us: forward_part(): attended = jnp.einsum('htk,khd->thd', rounded, value_rows, preferred_elem...]
    another operation x8 -> x0, local copies, waits for them, and re-layouts: 2.74 us -> none  [the longest x2 1.37 us: forward_part(): value_rows = memory_values.reshape(-1, heads_count, HEAD_DIM)]
  transfers between devices with their start and end apart: 5 -> 0, of which waited for: 4 -> 0; matrix products, arithmetic and copies ran while one was open for 11% -> 0% of each run, Pallas kernels for 0% -> 0%
where the time goes in v2:
time: 67.9 us; the launch traced here: 67.6 us
  Pallas kernels  66.9 us (99%)
    pallas_call x1, Pallas kernels, local(): pl.pallas_call(functools.partial(main_kernel, blk, picks), out_shape=(wid...  48.9 us
    pallas_call x1, Pallas kernels, local(): pl.pallas_call(write_kernel, out_shape=(wide, wide, small, small), in_spe...  18 us

profile of v2, /device:TPU:56, one launch (start us, length us, event | category | flops | bytes accessed | tf_op | source)
XLA Modules:
  0.0 67.6 jit_solution(2764079334613249752)
XLA Ops:
  0.6 48.9 %shard_map.102 = (bf16[512,512]{1,0:T(8,128)(2,1)}, bf16[2,8,512]{2,1,0:T(8,128)(2,1)}, bf16[2,8,512]{2,1,0:T(8,128)(2,1)}) custom-call(bf16[512,512]{1,0:T(8,128)(2,1)} %bitcast.9, bf16[512,512]{1,0:T(8,128)(2,1)} %bitcast.10, bf16[512,512]{1,0:T(8,128)(2,1)} %bitcast.11, bf16[2,8,512]{2,1,0:T(8,128)(2,1)} %bitcast.12, bf16[2,8,512]{2,1,0:T(8,128)(2,1)} %bitcast.13, ...), custom_call_target="tpu_custom_call" | custom-call | tf_op jit(solution)/shard_map/pallas_call | solution.py:322
  49.5 18.0 %shard_map.103 = (bf16[512,512]{1,0:T(8,128)(2,1)}, bf16[512,512]{1,0:T(8,128)(2,1)}, bf16[2,8,512]{2,1,0:T(8,128)(2,1)}, bf16[2,8,512]{2,1,0:T(8,128)(2,1)}) custom-call(bf16[512,512]{1,0:T(8,128)(2,1)} %get-tuple-element.11.recv_ref, bf16[2,8,512]{2,1,0:T(8,128)(2,1)} %get-tuple-element.12.kg_ref, bf16[2,8,512]{2,1,0:T(8,128)(2,1)} %get-tuple-element.13.vg_ref), custom_call_target="tpu_custom_call" | custom-call | tf_op jit(solution)/shard_map/pallas_call | solution.py:361

commit v3 on v2

--- a/solution.py
+++ b/solution.py
@@ -19,7 +19,7 @@
 MESH = pl.DeviceIdType.MESH
 SIDES = ((0, 1), (1, -1))
 FAR = (6, 5, -5, 4, -4)
-VMEM_LIMIT = 60 << 20
+VMEM_LIMIT = 40 << 20
 
 
 def wait_for(ref, sem):
@@ -319,9 +319,14 @@
     in_vmem = pl.BlockSpec(memory_space=pltpu.VMEM)
     wide = jax.ShapeDtypeStruct((tokens, W), BF16)
     small = jax.ShapeDtypeStruct((n_blk, blk, W), BF16)
+    held = pltpu.VMEM((tokens, W), BF16)
+    held_small = pltpu.VMEM((n_blk, blk, W), BF16)
+    operands = (
+        stream_in[0], saved_in[0], grad_out[0], mem_keys[0], mem_values[0], owner_map, block_ids
+    )
     recv, kg, vg = pl.pallas_call(
         functools.partial(main_kernel, blk, picks),
-        out_shape=(wide, small, small),
+        out_shape=(held, held_small, held_small),
         in_specs=[anywhere] * 7,
         out_specs=(anywhere, in_vmem, in_vmem),
         scratch_shapes=[
@@ -356,7 +361,7 @@
             collective_id=0, has_side_effects=True, vmem_limit_bytes=VMEM_LIMIT
         ),
     )(
-        stream_in[0], saved_in[0], grad_out[0], mem_keys[0], mem_values[0], owner_map, block_ids
+        *(pltpu.with_memory_space_constraint(operand, pltpu.HBM) for operand in operands)
     )
     outs = pl.pallas_call(
         write_kernel,

time: 67.9 us -> 50.2 us (0.74)
  Pallas kernels: 66.9 us -> 49.3 us
    pallas_call x1, Pallas kernels: 18 us -> 1.02 us  [local(): pl.pallas_call(write_kernel, out_shape=(wide, wide, small, small), in_spe...]
where the time goes in v3:
time: 50.2 us; the launch traced here: 50 us
  Pallas kernels  49.3 us (98%)
  between operations  0.64 us (1%)
    pallas_call x1, Pallas kernels, local(): pl.pallas_call(functools.partial(main_kernel, blk, picks), out_shape=(hel...  48.3 us
    pallas_call x1, Pallas kernels, local(): pl.pallas_call(write_kernel, out_shape=(wide, wide, small, small), in_spe...  1.02 us

profile of v3, /device:TPU:56, one launch (start us, length us, event | category | flops | bytes accessed | tf_op | source)
XLA Modules:
  0.0 50.0 jit_solution(14789098237262412569)
XLA Ops:
  0.6 48.3 %shard_map.102 = (bf16[512,512]{1,0:T(8,128)(2,1)S(1)}, bf16[2,8,512]{2,1,0:T(8,128)(2,1)S(1)}, bf16[2,8,512]{2,1,0:T(8,128)(2,1)S(1)}) custom-call(bf16[512,512]{1,0:T(8,128)(2,1)} %bitcast.9, bf16[512,512]{1,0:T(8,128)(2,1)} %bitcast.10, bf16[512,512]{1,0:T(8,128)(2,1)} %bitcast.11, bf16[2,8,512]{2,1,0:T(8,128)(2,1)} %bitcast.12, ...), custom_call_target="tpu_custom_call" | custom-call | tf_op jit(solution)/shard_map/pallas_call | solution.py:327
  48.9 1.0 %shard_map.103 = (bf16[512,512]{1,0:T(8,128)(2,1)}, bf16[512,512]{1,0:T(8,128)(2,1)}, bf16[2,8,512]{2,1,0:T(8,128)(2,1)}, bf16[2,8,512]{2,1,0:T(8,128)(2,1)}) custom-call(bf16[512,512]{1,0:T(8,128)(2,1)S(1)} %get-tuple-element.11.recv_ref, bf16[2,8,512]{2,1,0:T(8,128)(2,1)S(1)} %get-tuple-element.12.kg_ref, bf16[2,8,512]{2,1,0:T(8,128)(2,1)S(1)} %get-tuple-element.13.vg_ref), custom_call_target="tpu_custom_call" | custom-call | tf_op jit(solution)/shard_map/pallas_call | solution.py:366

commit v4 on v3

--- a/solution.py
+++ b/solution.py
@@ -30,9 +30,9 @@
     blk, picks,
     stream_ref, saved_ref, grad_ref, mk_ref, mv_ref, om_ref, ids_ref,
     recv_ref, kg_ref, vg_ref,
-    stream_v, saved_v, grad_v, mem_v, tab, G, S, C, pick, spread, kvb, kvf, terms, gs, res,
+    stream_v, saved_v, grad_v, saved_t, grad_t, mem_v, tab, G, D, S, C, pick, spread, kvb, kvf, terms, gs, res,
     T, rx, U, rr, rf, om_s, ids_s, tab_s,
-    load_sem, small_sem, tab_send, tab_recv, tab_sem, agz, agx, agz_send, agx_send,
+    load_sem, small_sem, tab_send, tab_recv, tab_sem, agz, agd, agx, agz_send, agx_send,
     rsx, rsr, rsf, rsx_send, rsz_send, pipe_send, pipe_recv,
 ):
     pipe, dp, ten = lax.axis_index("pipe"), lax.axis_index("dp"), lax.axis_index("tensor")
@@ -81,6 +81,12 @@
     for copy in loads:
         copy.start()
 
+    for copy in mem_loads:
+        copy.wait()
+    for i in range(2):
+        own = jnp.concatenate([mem_v[0, i].astype(F32), mem_v[1, i].astype(F32)], axis=0)
+        G[z, i] = own.astype(BF16)
+
     for copy in id_loads:
         copy.wait()
     places = [[om_s[ids_s[m, 0, 0, j]] for j in range(picks)] for m in range(2)]
@@ -91,17 +97,14 @@
         for j in range(picks):
             wanted = jnp.where(lane == owners[m][j], places[m][j] % 2, wanted)
     tab[0] = wanted
-    for copy in mem_loads:
-        copy.wait()
-    for i in range(2):
-        own = jnp.concatenate([mem_v[0, i].astype(F32), mem_v[1, i].astype(F32)], axis=0)
-        G[z, i] = own.astype(BF16)
     pl.semaphore_wait(barrier, len(partners) + 1)
 
-    for dz in (3, -3, 2, -2, 1, -1):
-        send(G.at[z], G.at[z], agz_send, agz.at[(-dz) % Z], dz, 0)
     for dx in range(1, X):
         send(tab.at[0], tab.at[X - dx], tab_send, tab_recv.at[X - dx - 1], 0, dx)
+    for dz in (1, -1, 3, -3, 2, -2):
+        send(G.at[z], G.at[z], agz_send, agz.at[(-dz) % Z], dz, 0)
+    for dx in (2, 1, 3):
+        send(G.at[z], D.at[X - dx - 1], agx_send, agd.at[X - dx - 1], 0, dx)
 
     ramp = lax.broadcasted_iota(jnp.int32, (blk, total), 1) - lax.broadcasted_iota(
         jnp.int32, (blk, total), 0
@@ -120,23 +123,16 @@
         wait_for(tab.at[dx], tab_recv.at[dx - 1])
     to_scalars = pltpu.make_async_copy(tab, tab_s, tab_sem)
     to_scalars.start()
-    for d, sg in SIDES:
-        far = G.at[zat(-3 * sg)]
-        wait_for(far, agz.at[(-3 * sg) % Z])
-        send(far, far, agz_send, agz.at[(-4 * sg) % Z], sg, 0)
-        send(far, far, agz_send, agz.at[(-5 * sg) % Z], 2 * sg, 0)
-        part = G.at[zat(-3 * sg), d]
-        send(part, part, agz_send, agz.at[6 + d * Z], 3 * sg, 0)
     to_scalars.wait()
 
     def slot(dx, o):
         return tab_s[dx, 0, at(o, 0)]
 
-    for o in (0, 3, -3, 1, -1, 2, -2, 4, -4, 5, -5, 6):
+    def to_peers(o):
         if o == 6:
             for d, _ in SIDES:
                 wait_for(G.at[zat(6), d], agz.at[6 + d * Z])
-        elif abs(o) not in (0, 3):
+        elif abs(o) != 3:
             wait_for(G.at[zat(o)], agz.at[o % Z])
         first, second = G[zat(o), 0], G[zat(o), 1]
         for dx in (2, 1, 3):
@@ -146,6 +142,33 @@
             )
         C[at(o, 0)] = jnp.where(slot(0, o) == 1, second, first)
 
+    to_peers(1)
+    to_peers(-1)
+    for d, sg in SIDES:
+        far = G.at[zat(-3 * sg)]
+        wait_for(far, agz.at[(-3 * sg) % Z])
+        send(far, far, agz_send, agz.at[(-4 * sg) % Z], sg, 0)
+        send(far, far, agz_send, agz.at[(-5 * sg) % Z], 2 * sg, 0)
+        part = G.at[zat(-3 * sg), d]
+        send(part, part, agz_send, agz.at[6 + d * Z], 3 * sg, 0)
+    for o in (3, -3, 2, -2):
+        to_peers(o)
+    C[dp] = jnp.where(slot(0, 0) == 1, G[z, 1], G[z, 0])
+    for dx in range(1, X):
+        wait_for(D.at[dx - 1], agd.at[dx - 1])
+        mine = tab_s[0, 0, at(0, dx)]
+        C[at(0, dx)] = jnp.where(mine == 1, D[dx - 1, 1], D[dx - 1, 0])
+    for copy in loads:
+        copy.wait()
+    for h in range(heads // 2):
+        cut = slice(h * HEAD, (h + 1) * HEAD)
+        saved_t[h], grad_t[h] = saved_v[:, cut].T, grad_v[:, cut].T
+    for o in (4, -4, 5, -5, 6):
+        to_peers(o)
+    for h in range(heads // 2, heads):
+        cut = slice(h * HEAD, (h + 1) * HEAD)
+        saved_t[h], grad_t[h] = saved_v[:, cut].T, grad_v[:, cut].T
+
     column = lax.broadcasted_iota(jnp.int32, (1, 2 * keys), 1)
     target = column % blk + jnp.where(column >= keys, blk, 0)
     for j in range(picks):
@@ -153,9 +176,7 @@
     hits = lax.broadcasted_iota(jnp.int32, (total, 2 * keys), 0) == target
     spread[...] = jnp.where(hits, 1.0, 0.0).astype(BF16)
 
-    for copy in loads:
-        copy.wait()
-    for o in (0, 3, -3, 1, -1, 2, -2, 4, -4, 5, -5, 6):
+    for o in (1, -1, 3, -3, 2, -2, 4, -4, 5, -5, 6):
         for dx in range(1, X):
             wait_for(C.at[at(o, dx)], agx.at[dx - 1, o % Z])
 
@@ -164,31 +185,45 @@
             pick[m], C[...].reshape(total, W), preferred_element_type=F32
         ).astype(BF16)
 
-    def softmax_t(k_h, q_h):
-        st = lax.dot_general(k_h, q_h, NT, preferred_element_type=F32) * scale
-        e = jnp.exp(st - jnp.max(st, axis=0, keepdims=True))
-        return e * (1.0 / jnp.sum(e, axis=0, keepdims=True))
+    def powers(st):
+        return jnp.exp2((st - jnp.max(st, axis=0, keepdims=True)) * (scale * math.log2(math.e)))
+
+    def backward_head(h):
+        cut = slice(h * HEAD, (h + 1) * HEAD)
+        e = powers(jnp.dot(kvb[0:keys, cut], saved_t[h], preferred_element_type=F32))
+        gw = jnp.dot(kvb[keys:, cut], grad_t[h], preferred_element_type=F32)
+        share = 1.0 / jnp.sum(e, axis=0, keepdims=True)
+        centre = jnp.sum(e * gw, axis=0, keepdims=True) * share
+        gst = (e * (share * scale) * (gw - centre)).astype(BF16)
+        gs[h] = gst
+        terms[0:keys, cut] = jnp.dot(
+            gst, saved_v[:, cut], preferred_element_type=F32
+        ).astype(BF16)
+        terms[keys:, cut] = jnp.dot(
+            (e * share).astype(BF16), grad_v[:, cut], preferred_element_type=F32
+        ).astype(BF16)
+
+    def to_column(o, part):
+        index = o % Z if part is None else o % Z + part * Z
+        cols = slice(0, W) if part is None else slice(part * W // 2, (part + 1) * W // 2)
+        for dx in (2, 1, 3):
+            send(
+                T.at[at(o, dx), :, cols], rx.at[X - dx - 1, o % Z, :, cols],
+                rsx_send, rsx.at[X - dx - 1, index], 0, dx,
+            )
 
     kvb[...] = select(1)
-    for h in range(heads):
-        cut = slice(h * HEAD, (h + 1) * HEAD)
-        q_h, g_h = saved_v[:, cut], grad_v[:, cut]
-        w = softmax_t(kvb[0:keys, cut], q_h)
-        gw = lax.dot_general(kvb[keys:, cut], g_h, NT, preferred_element_type=F32)
-        centre = jnp.sum(w * gw, axis=0, keepdims=True)
-        gst = (w * (gw - centre) * scale).astype(BF16)
-        gs[h] = gst
-        terms[0:keys, cut] = jnp.dot(gst, q_h, preferred_element_type=F32).astype(BF16)
-        terms[keys:, cut] = jnp.dot(
-            w.astype(BF16), g_h, preferred_element_type=F32
-        ).astype(BF16)
-    T[...] = jnp.dot(spread[...], terms[...], preferred_element_type=F32).astype(BF16).reshape(
-        Z * X, both, W
-    )
-
-    for o in FAR + (3, -3, 2, -2, 1, -1, 0):
-        for dx in (2, 1, 3):
-            send(T.at[at(o, dx)], rx.at[X - dx - 1, o % Z], rsx_send, rsx.at[X - dx - 1, o % Z], 0, dx)
+    for part in range(2):
+        for h in range(part * heads // 2, (part + 1) * heads // 2):
+            backward_head(h)
+        cols = slice(part * W // 2, (part + 1) * W // 2)
+        T[:, :, cols] = jnp.dot(
+            spread[...], terms[:, cols], preferred_element_type=F32
+        ).astype(BF16).reshape(Z * X, both, W // 2)
+        for o in FAR:
+            to_column(o, part)
+    for o in (3, -3, 2, -2, 1, -1, 0):
+        to_column(o, None)
 
     def exchange():
         return pltpu.make_async_remote_copy(
@@ -202,7 +237,8 @@
         for h in range(heads):
             cut = slice(h * HEAD, (h + 1) * HEAD)
             s_h = stream_v[:, cut]
-            w = softmax_t(kvf[0:keys, cut], s_h).astype(BF16)
+            e = powers(lax.dot_general(kvf[0:keys, cut], s_h, NT, preferred_element_type=F32))
+            w = (e * (1.0 / jnp.sum(e, axis=0, keepdims=True))).astype(BF16)
             out = lax.dot_general(w, kvf[keys:, cut], TN, preferred_element_type=F32)
             res[:, cut] = (s_h.astype(F32) + out).astype(BF16)
 
@@ -217,7 +253,12 @@
 
     def combine(o):
         for dx in range(1, X):
-            wait_for(rx.at[dx - 1, o % Z], rsx.at[dx - 1, o % Z])
+            if o in FAR:
+                for part in range(2):
+                    cols = slice(part * W // 2, (part + 1) * W // 2)
+                    wait_for(rx.at[dx - 1, o % Z, :, cols], rsx.at[dx - 1, o % Z + part * Z])
+            else:
+                wait_for(rx.at[dx - 1, o % Z], rsx.at[dx - 1, o % Z])
         sums = [None, None]
         for dx in range(X):
             part = (T[at(o, 0)] if dx == 0 else rx[dx - 1, o % Z]).astype(F32)
@@ -271,7 +312,7 @@
     wait_for(tab.at[0:X - 1], tab_send)
     wait_for(G.at[0:Z - 1], agz_send)
     wait_for(U.at[0:Z - 1], rsz_send)
-    wait_for(C.at[0:(X - 1) * Z], agx_send)
+    wait_for(C.at[0:(X - 1) * (Z + 1)], agx_send)
     wait_for(T.at[0:(X - 1) * Z], rsx_send)
     wait_for(res, pipe_send)
     wait_for(res, pipe_recv)
@@ -333,9 +374,12 @@
             pltpu.VMEM((tokens, W), BF16),
             pltpu.VMEM((tokens, W), BF16),
             pltpu.VMEM((tokens, W), BF16),
+            pltpu.VMEM((heads, HEAD, tokens), BF16),
+            pltpu.VMEM((heads, HEAD, tokens), BF16),
             pltpu.VMEM((2, n_blk, blk, W), BF16),
             pltpu.VMEM((X, 8, LANES), jnp.int32),
             pltpu.VMEM((Z, 2, both, W), BF16),
+            pltpu.VMEM((X - 1, 2, both, W), BF16),
             pltpu.VMEM((X - 1, Z, both, W), BF16),
             pltpu.VMEM((Z * X, both, W), BF16),
             pltpu.VMEM((2, 2 * keys, Z * X * both), BF16),
@@ -354,8 +398,8 @@
             pltpu.SMEM(block_ids.shape, jnp.int32),
             pltpu.SMEM((X, 8, LANES), jnp.int32),
             DMA((3,)), DMA((4,)), DMA(()), DMA((X - 1,)), DMA(()),
-            DMA((2 * Z,)), DMA((X - 1, Z)), DMA(()), DMA(()),
-            DMA((X - 1, Z)), DMA((2, 3)), DMA((2, 3)), DMA(()), DMA(()), DMA(()), DMA(()),
+            DMA((2 * Z,)), DMA((X - 1,)), DMA((X - 1, Z)), DMA(()), DMA(()),
+            DMA((X - 1, 2 * Z)), DMA((2, 3)), DMA((2, 3)), DMA(()), DMA(()), DMA(()), DMA(()),
         ],
         compiler_params=pltpu.CompilerParams(
             collective_id=0, has_side_effects=True, vmem_limit_bytes=VMEM_LIMIT

time: 50.2 us -> 49.9 us (level)
  no operation moved by 1% of the time
where the time goes in v4:
time: 49.9 us; the launch traced here: 49.7 us
  Pallas kernels  49.1 us (98%)
  between operations  0.64 us (1%)
    pallas_call x1, Pallas kernels, local(): pl.pallas_call(functools.partial(main_kernel, blk, picks), out_shape=(hel...  48.1 us
    pallas_call x1, Pallas kernels, local(): pl.pallas_call(write_kernel, out_shape=(wide, wide, small, small), in_spe...  1.02 us

profile of v4, /device:TPU:56, one launch (start us, length us, event | category | flops | bytes accessed | tf_op | source)
XLA Modules:
  0.0 49.7 jit_solution(4448045512047366294)
XLA Ops:
  0.6 48.1 %shard_map.102 = (bf16[512,512]{1,0:T(8,128)(2,1)S(1)}, bf16[2,8,512]{2,1,0:T(8,128)(2,1)S(1)}, bf16[2,8,512]{2,1,0:T(8,128)(2,1)S(1)}) custom-call(bf16[512,512]{1,0:T(8,128)(2,1)} %bitcast.9, bf16[512,512]{1,0:T(8,128)(2,1)} %bitcast.10, bf16[512,512]{1,0:T(8,128)(2,1)} %bitcast.11, bf16[2,8,512]{2,1,0:T(8,128)(2,1)} %bitcast.12, ...), custom_call_target="tpu_custom_call" | custom-call | tf_op jit(solution)/shard_map/pallas_call | solution.py:368
  48.7 1.0 %shard_map.103 = (bf16[512,512]{1,0:T(8,128)(2,1)}, bf16[512,512]{1,0:T(8,128)(2,1)}, bf16[2,8,512]{2,1,0:T(8,128)(2,1)}, bf16[2,8,512]{2,1,0:T(8,128)(2,1)}) custom-call(bf16[512,512]{1,0:T(8,128)(2,1)S(1)} %get-tuple-element.11.recv_ref, bf16[2,8,512]{2,1,0:T(8,128)(2,1)S(1)} %get-tuple-element.12.kg_ref, bf16[2,8,512]{2,1,0:T(8,128)(2,1)S(1)} %get-tuple-element.13.vg_ref), custom_call_target="tpu_custom_call" | custom-call | tf_op jit(solution)/shard_map/pallas_call | solution.py:410

commit v5 on v4

--- a/solution.py
+++ b/solution.py
@@ -222,7 +222,7 @@
         ).astype(BF16).reshape(Z * X, both, W // 2)
         for o in FAR:
             to_column(o, part)
-    for o in (3, -3, 2, -2, 1, -1, 0):
+    for o in (2, -2, 1, -1, 3, -3, 0):
         to_column(o, None)
 
     def exchange():
@@ -290,16 +290,15 @@
             o = sg * (4 + k)
             keep(o)
             send(U.at[o % Z], rr.at[d, k], rsz_send, rsr.at[d, k], sg * (k + 1), 0)
+    for k in (1, 0):
+        for d, sg in SIDES:
+            o = sg * (k + 1)
+            keep(o)
+            send(U.at[o % Z], rf.at[d, k], rsz_send, rsf.at[d, k], o, 0)
     for d, sg in SIDES:
         keep(3 * sg)
     for d, sg in SIDES:
-        keep(2 * sg)
-        send(U.at[(2 * sg) % Z], rf.at[d, 1], rsz_send, rsf.at[d, 1], 2 * sg, 0)
-    for d, sg in SIDES:
         relay(d, sg)
-    for d, sg in SIDES:
-        keep(sg)
-        send(U.at[sg % Z], rf.at[d, 0], rsz_send, rsf.at[d, 0], sg, 0)
     last = combine(0)
     for k in range(3):
         for d, sg in SIDES:

time: 49.9 us -> 49.9 us (level)
  no operation moved by 1% of the time
where the time goes in v5:
time: 49.9 us; the launch traced here: 49.6 us
  Pallas kernels  49 us (98%)
  between operations  0.64 us (1%)
    pallas_call x1, Pallas kernels, local(): pl.pallas_call(functools.partial(main_kernel, blk, picks), out_shape=(hel...  48 us
    pallas_call x1, Pallas kernels, local(): pl.pallas_call(write_kernel, out_shape=(wide, wide, small, small), in_spe...  1.02 us

profile of v5, /device:TPU:56, one launch (start us, length us, event | category | flops | bytes accessed | tf_op | source)
XLA Modules:
  0.0 49.6 jit_solution(16735498093013027794)
XLA Ops:
  0.6 48.0 %shard_map.102 = (bf16[512,512]{1,0:T(8,128)(2,1)S(1)}, bf16[2,8,512]{2,1,0:T(8,128)(2,1)S(1)}, bf16[2,8,512]{2,1,0:T(8,128)(2,1)S(1)}) custom-call(bf16[512,512]{1,0:T(8,128)(2,1)} %bitcast.9, bf16[512,512]{1,0:T(8,128)(2,1)} %bitcast.10, bf16[512,512]{1,0:T(8,128)(2,1)} %bitcast.11, bf16[2,8,512]{2,1,0:T(8,128)(2,1)} %bitcast.12, ...), custom_call_target="tpu_custom_call" | custom-call | tf_op jit(solution)/shard_map/pallas_call | solution.py:367
  48.6 1.0 %shard_map.103 = (bf16[512,512]{1,0:T(8,128)(2,1)}, bf16[512,512]{1,0:T(8,128)(2,1)}, bf16[2,8,512]{2,1,0:T(8,128)(2,1)}, bf16[2,8,512]{2,1,0:T(8,128)(2,1)}) custom-call(bf16[512,512]{1,0:T(8,128)(2,1)S(1)} %get-tuple-element.11.recv_ref, bf16[2,8,512]{2,1,0:T(8,128)(2,1)S(1)} %get-tuple-element.12.kg_ref, bf16[2,8,512]{2,1,0:T(8,128)(2,1)S(1)} %get-tuple-element.13.vg_ref), custom_call_target="tpu_custom_call" | custom-call | tf_op jit(solution)/shard_map/pallas_call | solution.py:409

commit v6 on v5

--- a/solution.py
+++ b/solution.py
@@ -101,7 +101,7 @@
 
     for dx in range(1, X):
         send(tab.at[0], tab.at[X - dx], tab_send, tab_recv.at[X - dx - 1], 0, dx)
-    for dz in (1, -1, 3, -3, 2, -2):
+    for dz in (3, -3, 1, -1, 2, -2):
         send(G.at[z], G.at[z], agz_send, agz.at[(-dz) % Z], dz, 0)
     for dx in (2, 1, 3):
         send(G.at[z], D.at[X - dx - 1], agx_send, agd.at[X - dx - 1], 0, dx)
@@ -142,8 +142,6 @@
             )
         C[at(o, 0)] = jnp.where(slot(0, o) == 1, second, first)
 
-    to_peers(1)
-    to_peers(-1)
     for d, sg in SIDES:
         far = G.at[zat(-3 * sg)]
         wait_for(far, agz.at[(-3 * sg) % Z])
@@ -151,6 +149,8 @@
         send(far, far, agz_send, agz.at[(-5 * sg) % Z], 2 * sg, 0)
         part = G.at[zat(-3 * sg), d]
         send(part, part, agz_send, agz.at[6 + d * Z], 3 * sg, 0)
+    to_peers(1)
+    to_peers(-1)
     for o in (3, -3, 2, -2):
         to_peers(o)
     C[dp] = jnp.where(slot(0, 0) == 1, G[z, 1], G[z, 0])

time: 49.9 us -> 49.1 us (0.984)
  Pallas kernels: 49 us -> 48.3 us
    pallas_call x1, Pallas kernels: 48 us -> 47.3 us  [local(): pl.pallas_call(functools.partial(main_kernel, blk, picks), out_shape=(hel...]
where the time goes in v6:
time: 49.1 us; the launch traced here: 48.9 us
  Pallas kernels  48.3 us (98%)
  between operations  0.64 us (1%)
    pallas_call x1, Pallas kernels, local(): pl.pallas_call(functools.partial(main_kernel, blk, picks), out_shape=(hel...  47.3 us
    pallas_call x1, Pallas kernels, local(): pl.pallas_call(write_kernel, out_shape=(wide, wide, small, small), in_spe...  1.02 us

profile of v6, /device:TPU:56, one launch (start us, length us, event | category | flops | bytes accessed | tf_op | source)
XLA Modules:
  0.0 48.9 jit_solution(16871692567682619621)
XLA Ops:
  0.6 47.3 %shard_map.102 = (bf16[512,512]{1,0:T(8,128)(2,1)S(1)}, bf16[2,8,512]{2,1,0:T(8,128)(2,1)S(1)}, bf16[2,8,512]{2,1,0:T(8,128)(2,1)S(1)}) custom-call(bf16[512,512]{1,0:T(8,128)(2,1)} %bitcast.9, bf16[512,512]{1,0:T(8,128)(2,1)} %bitcast.10, bf16[512,512]{1,0:T(8,128)(2,1)} %bitcast.11, bf16[2,8,512]{2,1,0:T(8,128)(2,1)} %bitcast.12, ...), custom_call_target="tpu_custom_call" | custom-call | tf_op jit(solution)/shard_map/pallas_call | solution.py:367
  47.9 1.0 %shard_map.103 = (bf16[512,512]{1,0:T(8,128)(2,1)}, bf16[512,512]{1,0:T(8,128)(2,1)}, bf16[2,8,512]{2,1,0:T(8,128)(2,1)}, bf16[2,8,512]{2,1,0:T(8,128)(2,1)}) custom-call(bf16[512,512]{1,0:T(8,128)(2,1)S(1)} %get-tuple-element.11.recv_ref, bf16[2,8,512]{2,1,0:T(8,128)(2,1)S(1)} %get-tuple-element.12.kg_ref, bf16[2,8,512]{2,1,0:T(8,128)(2,1)S(1)} %get-tuple-element.13.vg_ref), custom_call_target="tpu_custom_call" | custom-call | tf_op jit(solution)/shard_map/pallas_call | solution.py:409
